TPU v7x, 768 devices: a whole 4x8x12 slice. The times are simulated.
768 devices in a mesh: brick: 48 (over y, z_lo), level: 16 (over x, z_hi, core).
Axes of the slice: x: 4, y: 8, z: 12 (z_hi: 2, z_lo: 6; z = z_hi * 6 + z_lo), core: 2. Of those that a mesh axis runs over, the one named last changes fastest.
Arguments:
- adjoint: float32 [5, 128, 384, 128], P(None, 'level', 'brick'), may hold values from -6 to 6
- source: float32 [5, 128, 384, 128], P(None, 'level', 'brick'), may hold values from -48 to 48
- block: bfloat16 [5, 5, 128, 384, 128], P(None, None, 'level', 'brick'), may hold values from -1 to 13
- precond: bfloat16 [5, 5, 128, 384, 128], P(None, None, 'level', 'brick'), may hold values from -0.01 to 0.14
- couple: float32 [3, 128, 384, 128], P(None, 'level', 'brick'), may hold values from 0.1 to 0.6
- solid: int32 [128, 384, 128], P('level', 'brick'), may hold values 0 or 1
- coarse_owner: int32 [16], replicated, may hold values from 0 to 15, each once
Outputs:
- smoothed: float32 [5, 128, 384, 128], P(None, 'level', 'brick')
- coarse_rhs: float32 [16, 5, 64, 192, 4], P('level', None, None, 'brick')
Inputs may be any that keep to these rules, and one draw needn't show every extreme that they name: `coarse_owner`: each level index owns exactly one block.
All inputs are finite; a program needn't handle non-finite values. No bound on the sum of `solid` on one device may be relied on, other than what follows from the above.
Results may differ from a plain program's by a relative error of at most 0.0003.
Values may be sent and summed in bfloat16 or wider, within the bound.
No kernel may reach another device: no remote copies, remote signals or barrier semaphores. Data moves between devices by JAX's collectives and lax.ppermute only.
A program may use at most 32 MiB of HBM per device.

v0:
```python
import jax
import jax.numpy as jnp
from jax import lax
from jax.sharding import PartitionSpec as P

SWEEPS = 4


relax_factor = 0.8


def extended(cells, sides, width):
    for axis, dim in sides:
        count = lax.axis_size(axis)
        ends = count - 1
        head = lax.slice_in_dim(cells, 0, width, axis=dim)
        tail = lax.slice_in_dim(cells, cells.shape[dim] - width, cells.shape[dim], axis=dim)
        cells = jnp.concatenate(
            [
                lax.ppermute(tail, axis, [(i, (i + 1) % count) for i in range(ends)]),
                cells,
                lax.ppermute(head, axis, [((i + 1) % count, i) for i in range(ends)]),
            ],
            axis=dim,
        )
    return cells


def passed_along(block, axis, distance):
    devices = range(lax.axis_size(axis))
    route = [(i - distance, i) for i in devices if i - distance in devices]
    return lax.ppermute(block, axis, route)


def apply_operator(padded, block, couple):
    center = padded[:, 1:-1, 1:-1, :]
    count = center.shape[0]
    fields = []
    for outer in range(count):
        total = block[0, outer].astype(jnp.float32) * center[0]
        for inner in range(1, count):
            total = total + block[inner, outer].astype(jnp.float32) * center[inner]
        fields.append(total)
    diagonal_part = jnp.stack(fields)
    across_x = padded[:, 2:, 1:-1, :] + padded[:, :-2, 1:-1, :]
    across_y = padded[:, 1:-1, 2:, :] + padded[:, 1:-1, :-2, :]
    zero_plane = jnp.zeros_like(center[..., :1])
    across_z = jnp.concatenate([center[..., 1:], zero_plane], -1) + jnp.concatenate(
        [zero_plane, center[..., :-1]], -1
    )
    coupled = couple[0] * across_x + couple[1] * across_y + couple[2] * across_z
    return diagonal_part - coupled


def precondition(precond, defect):
    count = defect.shape[0]
    fields = []
    for outer in range(count):
        total = precond[outer, 0].astype(jnp.float32) * defect[0]
        for inner in range(1, count):
            total = total + precond[outer, inner].astype(jnp.float32) * defect[inner]
        fields.append(total)
    return jnp.stack(fields)


def restrict_along(field, axis, before):
    length = field.shape[axis]
    even = lax.slice_in_dim(field, 0, length, 2, axis)
    odd = lax.slice_in_dim(field, 1, length, 2, axis)
    earlier = jnp.concatenate(
        [before, lax.slice_in_dim(odd, 0, odd.shape[axis] - 1, 1, axis)], axis
    )
    return 0.5 * even + 0.25 * odd + 0.25 * earlier


def zero_first(field, axis):
    return jnp.zeros_like(lax.slice_in_dim(field, 0, 1, 1, axis))


def extend(field):
    return extended(field, (("brick", 2), ("level", 1)), 1)


def shards(adjoint, source, block, precond, couple, solid, coarse_owner):
    keep = solid == 0
    smoothed = adjoint
    for sweep in range(SWEEPS):
        defect = source - apply_operator(extend(smoothed), block, couple)
        smoothed = jnp.where(keep, smoothed + relax_factor * precondition(precond, defect), 0.0)
    residual = jnp.where(keep, source - apply_operator(extend(smoothed), block, couple), 0.0)
    coarse_z = restrict_along(residual, 3, zero_first(residual, 3))
    below = passed_along(coarse_z[:, :, -1:, :], "brick", 1)
    coarse_y = restrict_along(coarse_z, 2, below)
    own_part = restrict_along(coarse_y, 1, zero_first(coarse_y, 1))
    edge_row = 0.25 * coarse_y[:, -1:]
    partial_value = jnp.concatenate([own_part, edge_row], 1)
    count = partial_value.shape[0]
    half_x = own_part.shape[1]
    half_y = partial_value.shape[2]
    levels = lax.axis_size("level")
    zblock = partial_value.shape[3] // levels
    split = partial_value.reshape(count, half_x + 1, half_y, levels, zblock)
    slots = jnp.arange(levels, dtype=jnp.int32)
    inverse = jnp.sum(jnp.where(coarse_owner[None, :] == slots[:, None], slots[None, :], 0), axis=1)
    ordered = jnp.moveaxis(jnp.take(split, inverse, axis=3), 3, 0)
    received = lax.all_to_all(ordered, "level", split_axis=0, concat_axis=0, tiled=True)
    own_blocks = received[:, :, :half_x]
    edges = received[:, :, half_x]
    shifted = jnp.concatenate([jnp.zeros_like(edges[:1]), edges[:-1]], 0)
    first = own_blocks[:, :, :1] + shifted[:, :, None]
    own_blocks = jnp.concatenate([first, own_blocks[:, :, 1:]], 2)
    coarse_rhs = own_blocks.transpose(1, 0, 2, 3, 4).reshape(
        count, levels * half_x, half_y, zblock
    )[None]
    return (smoothed, coarse_rhs)


def solution(mesh):
    placed = (
        P(None, "level", "brick", None),
        P(None, "level", "brick", None),
        P(None, None, "level", "brick", None),
        P(None, None, "level", "brick", None),
        P(None, "level", "brick", None),
        P("level", "brick", None),
        P(),
    )
    return jax.shard_map(
        shards,
        mesh=mesh,
        in_specs=placed,
        out_specs=(P(None, "level", "brick", None), P("level", None, None, "brick", None)),
        check_vma=False,
    )
```

profile of v0, /device:TPU:33, one launch (start us, length us, event | category | flops | bytes accessed | tf_op | source)
XLA Modules:
  0.0 213.2 jit_solution(14406051610718545805)
XLA Ops:
  0.6 1.0 fusion.232
  1.7 12.3 %collective-permute-start.1 = (f32[5,8,1,128]{3,2,1,0:T(1,128)S(1)}, f32[5,8,1,128]{3,2,1,0:T(1,128)S(1)}, u32[]{:S(2)}, u32[]{:S(2)}) collective-permute-start(f32[5,8,1,128]{3,2,1,0:T(1,128)S(1)} %get-tuple-element.30), channel_id=1, source_target_pairs={{16,0},{32,16},{48,32},{64,48},{80,64},{96,80},{112,96},{128,112},... | collective-permute-start | bytes 61448 | tf_op jit(solution)/shard_map/ppermute | solution.py:22
  14.0 2.1 collective-permute-start
  16.1 1.1 fusion.231
  17.3 0.1 select_reduce_fusion
  17.4 0.7 copy-done
  18.3 7.3 %collective-permute-done = f32[5,8,1,128]{3,2,1,0:T(1,128)S(1)} collective-permute-done((f32[5,8,1,128]{3,2,1,0:T(1,128)S(1)}, f32[5,8,1,128]{3,2,1,0:T(1,128)S(1)}, u32[]{:S(2)}, u32[]{:S(2)}) %collective-permute-start) | collective-permute-done | bytes 20512 | tf_op jit(solution)/shard_map/ppermute | solution.py:20
  25.6 4.0 %collective-permute-start.2 = (f32[5,1,10,128]{3,2,1,0:T(8,128)S(1)}, f32[5,1,10,128]{3,2,1,0:T(8,128)S(1)}, u32[]{:S(2)}, u32[]{:S(2)}) collective-permute-start(f32[5,1,10,128]{3,2,1,0:T(8,128)S(1)} %get-tuple-element.10), channel_id=1, source_target_pairs={{1,0},{2,1},{3,2},{4,3},{5,4},{6,5},{7,6},{8,7},{9,8},{10,9},{11,1... | collective-permute-start | bytes 76808 | tf_op jit(solution)/shard_map/ppermute | solution.py:22
  29.7 9.7 %collective-permute-start.3 = (f32[5,1,10,128]{3,2,1,0:T(8,128)S(1)}, f32[5,1,10,128]{3,2,1,0:T(8,128)S(1)}, u32[]{:S(2)}, u32[]{:S(2)}) collective-permute-start(f32[5,1,10,128]{3,2,1,0:T(8,128)S(1)} %get-tuple-element.11), channel_id=1, source_target_pairs={{0,1},{1,2},{2,3},{3,4},{4,5},{5,6},{6,7},{7,8},{8,9},{9,10},{10,1... | collective-permute-start | bytes 76808 | tf_op jit(solution)/shard_map/ppermute | solution.py:20
  39.3 1.1 collective-permute-done.3
  40.4 0.2 fusion.38
  40.6 0.8 copy-done.3
  41.6 0.1 fusion.229
  41.8 1.9 collective-permute-start.5
  43.7 3.4 %collective-permute-start.4 = (f32[5,8,1,128]{3,2,1,0:T(1,128)S(1)}, f32[5,8,1,128]{3,2,1,0:T(1,128)S(1)}, u32[]{:S(2)}, u32[]{:S(2)}) collective-permute-start(f32[5,8,1,128]{3,2,1,0:T(1,128)S(1)} %get-tuple-element.27), channel_id=1, source_target_pairs={{0,16},{16,32},{32,48},{48,64},{64,80},{80,96},{96,112},{112,128},... | collective-permute-start | bytes 61448 | tf_op jit(solution)/shard_map/ppermute | solution.py:20
  47.1 8.0 %collective-permute-done.4 = f32[5,8,1,128]{3,2,1,0:T(1,128)S(1)} collective-permute-done((f32[5,8,1,128]{3,2,1,0:T(1,128)S(1)}, f32[5,8,1,128]{3,2,1,0:T(1,128)S(1)}, u32[]{:S(2)}, u32[]{:S(2)}) %collective-permute-start.4) | collective-permute-done | bytes 20512 | tf_op jit(solution)/shard_map/ppermute | solution.py:20
  55.2 1.9 collective-permute-start.6
  57.1 12.2 %collective-permute-start.7 = (f32[5,1,10,128]{3,2,1,0:T(8,128)S(1)}, f32[5,1,10,128]{3,2,1,0:T(8,128)S(1)}, u32[]{:S(2)}, u32[]{:S(2)}) collective-permute-start(f32[5,1,10,128]{3,2,1,0:T(8,128)S(1)} %get-tuple-element.9), channel_id=1, source_target_pairs={{0,1},{1,2},{2,3},{3,4},{4,5},{5,6},{6,7},{7,8},{8,9},{9,10},{10,1... | collective-permute-start | bytes 76808 | tf_op jit(solution)/shard_map/ppermute | solution.py:20
  69.3 1.0 collective-permute-done.7
  70.4 0.2 fusion.30
  70.8 0.1 fusion.227
  70.9 1.9 collective-permute-start.9
  72.8 3.4 %collective-permute-start.8 = (f32[5,8,1,128]{3,2,1,0:T(1,128)S(1)}, f32[5,8,1,128]{3,2,1,0:T(1,128)S(1)}, u32[]{:S(2)}, u32[]{:S(2)}) collective-permute-start(f32[5,8,1,128]{3,2,1,0:T(1,128)S(1)} %get-tuple-element.23), channel_id=1, source_target_pairs={{0,16},{16,32},{32,48},{48,64},{64,80},{80,96},{96,112},{112,128},... | collective-permute-start | bytes 61448 | tf_op jit(solution)/shard_map/ppermute | solution.py:20
  76.3 8.0 %collective-permute-done.8 = f32[5,8,1,128]{3,2,1,0:T(1,128)S(1)} collective-permute-done((f32[5,8,1,128]{3,2,1,0:T(1,128)S(1)}, f32[5,8,1,128]{3,2,1,0:T(1,128)S(1)}, u32[]{:S(2)}, u32[]{:S(2)}) %collective-permute-start.8) | collective-permute-done | bytes 20512 | tf_op jit(solution)/shard_map/ppermute | solution.py:20
  84.3 1.9 collective-permute-start.10
  86.2 11.7 %collective-permute-start.11 = (f32[5,1,10,128]{3,2,1,0:T(8,128)S(1)}, f32[5,1,10,128]{3,2,1,0:T(8,128)S(1)}, u32[]{:S(2)}, u32[]{:S(2)}) collective-permute-start(f32[5,1,10,128]{3,2,1,0:T(8,128)S(1)} %get-tuple-element.7), channel_id=1, source_target_pairs={{0,1},{1,2},{2,3},{3,4},{4,5},{5,6},{6,7},{7,8},{8,9},{9,10},{10,1... | collective-permute-start | bytes 76808 | tf_op jit(solution)/shard_map/ppermute | solution.py:20
  98.0 1.0 collective-permute-done.11
  99.0 0.2 fusion.22
  99.5 1.9 collective-permute-start.13
  101.4 3.4 %collective-permute-start.12 = (f32[5,8,1,128]{3,2,1,0:T(1,128)S(1)}, f32[5,8,1,128]{3,2,1,0:T(1,128)S(1)}, u32[]{:S(2)}, u32[]{:S(2)}) collective-permute-start(f32[5,8,1,128]{3,2,1,0:T(1,128)S(1)} %get-tuple-element.19), channel_id=1, source_target_pairs={{0,16},{16,32},{32,48},{48,64},{64,80},{80,96},{96,112},{112,128},... | collective-permute-start | bytes 61448 | tf_op jit(solution)/shard_map/ppermute | solution.py:20
  104.9 8.0 %collective-permute-done.12 = f32[5,8,1,128]{3,2,1,0:T(1,128)S(1)} collective-permute-done((f32[5,8,1,128]{3,2,1,0:T(1,128)S(1)}, f32[5,8,1,128]{3,2,1,0:T(1,128)S(1)}, u32[]{:S(2)}, u32[]{:S(2)}) %collective-permute-start.12) | collective-permute-done | bytes 20512 | tf_op jit(solution)/shard_map/ppermute | solution.py:20
  112.9 1.9 collective-permute-start.14
  114.8 11.7 %collective-permute-start.15 = (f32[5,1,10,128]{3,2,1,0:T(8,128)S(1)}, f32[5,1,10,128]{3,2,1,0:T(8,128)S(1)}, u32[]{:S(2)}, u32[]{:S(2)}) collective-permute-start(f32[5,1,10,128]{3,2,1,0:T(8,128)S(1)} %get-tuple-element.5), channel_id=1, source_target_pairs={{0,1},{1,2},{2,3},{3,4},{4,5},{5,6},{6,7},{7,8},{8,9},{9,10},{10,1... | collective-permute-start | bytes 76808 | tf_op jit(solution)/shard_map/ppermute | solution.py:20
  126.6 1.0 collective-permute-done.15
  127.6 0.2 fusion.14
  128.2 1.9 collective-permute-start.17
  130.1 3.4 %collective-permute-start.16 = (f32[5,8,1,128]{3,2,1,0:T(1,128)S(1)}, f32[5,8,1,128]{3,2,1,0:T(1,128)S(1)}, u32[]{:S(2)}, u32[]{:S(2)}) collective-permute-start(f32[5,8,1,128]{3,2,1,0:T(1,128)S(1)} %get-tuple-element.15), channel_id=1, source_target_pairs={{0,16},{16,32},{32,48},{48,64},{64,80},{80,96},{96,112},{112,128},... | collective-permute-start | bytes 61448 | tf_op jit(solution)/shard_map/ppermute | solution.py:20
  133.6 8.0 %collective-permute-done.16 = f32[5,8,1,128]{3,2,1,0:T(1,128)S(1)} collective-permute-done((f32[5,8,1,128]{3,2,1,0:T(1,128)S(1)}, f32[5,8,1,128]{3,2,1,0:T(1,128)S(1)}, u32[]{:S(2)}, u32[]{:S(2)}) %collective-permute-start.16) | collective-permute-done | bytes 20512 | tf_op jit(solution)/shard_map/ppermute | solution.py:20
  141.6 1.9 collective-permute-start.18
  143.5 11.7 %collective-permute-start.19 = (f32[5,1,10,128]{3,2,1,0:T(8,128)S(1)}, f32[5,1,10,128]{3,2,1,0:T(8,128)S(1)}, u32[]{:S(2)}, u32[]{:S(2)}) collective-permute-start(f32[5,1,10,128]{3,2,1,0:T(8,128)S(1)} %get-tuple-element.3), channel_id=1, source_target_pairs={{0,1},{1,2},{2,3},{3,4},{4,5},{5,6},{6,7},{7,8},{8,9},{9,10},{10,1... | collective-permute-start | bytes 76808 | tf_op jit(solution)/shard_map/ppermute | solution.py:20
  155.2 1.0 collective-permute-done.19
  156.3 0.2 fusion.6
  156.4 3.1 %slice.499 = f32[5,8,8,64]{3,2,1,0:T(8,128)S(1)} slice(f32[5,8,8,128]{3,2,1,0:T(8,128)S(1)} %fusion.6), slice={[0:5:1], [0:8:1], [0:8:1], [1:128:2]} | slice | bytes 163840 | tf_op jit(solution)/shard_map/slice | solution.py:69
  159.6 3.1 %slice.498 = f32[5,8,8,64]{3,2,1,0:T(8,128)S(1)} slice(f32[5,8,8,128]{3,2,1,0:T(8,128)S(1)} %fusion.6), slice={[0:5:1], [0:8:1], [0:8:1], [0:128:2]} | slice | bytes 163840 | tf_op jit(solution)/shard_map/slice | solution.py:68
  162.7 0.1 multiply_add_fusion
  162.8 1.9 collective-permute-start.20
  164.7 0.2 slice.502
  164.9 0.2 slice.501
  165.1 9.1 %collective-permute-done.20 = f32[5,8,1,64]{3,2,1,0:T(1,128)S(1)} collective-permute-done((f32[5,8,1,64]{3,2,1,0:T(1,128)S(1)}, f32[5,8,1,64]{3,2,1,0:T(1,128)S(1)}, u32[]{:S(2)}, u32[]{:S(2)}) %collective-permute-start.20) | collective-permute-done | bytes 10272 | tf_op jit(solution)/shard_map/ppermute | solution.py:32
  174.4 0.3 copy.45
  174.7 1.1 gather_fusion
  175.8 0.2 fusion.233
  176.0 0.9 reshape.861
  176.9 30.2 %all_to_all.5 = f32[16,1,400]{2,1,0:T(1,128)S(1)} all-to-all(f32[16,1,400]{2,1,0:T(1,128)S(1)} %reshape.861), channel_id=1, replica_groups=mesh['brick'=48,'level'=16] {'level'}, dimensions={0} | all-to-all | bytes 51200 | tf_op jit(solution)/shard_map/all_to_all | solution.py:106
  207.1 0.5 broadcast.101
  207.6 0.7 reduce
  208.4 0.7 reshape.862
  209.1 0.4 slice.1108
  209.4 0.4 slice.1109
  209.9 0.6 copy.46
  210.4 0.6 copy.42
  211.0 0.6 copy.43
  211.8 0.5 copy.44
  212.3 0.9 broadcast_in_dim_reshape.3
  (98 shorter events, 2.0 us)
Async XLA Ops:
  1.7 16.7 %collective-permute-start.1 = (f32[5,8,1,128]{3,2,1,0:T(1,128)S(1)}, f32[5,8,1,128]{3,2,1,0:T(1,128)S(1)}, u32[]{:S(2)}, u32[]{:S(2)}) collective-permute-start(f32[5,8,1,128]{3,2,1,0:T(1,128)S(1)} %get-tuple-element.30), channel_id=1, source_target_pairs={{16,0},{32,16},{48,32},{64,48},{80,64},{96,80},{112,96},{128,112},... | collective-permute-start | bytes 61448 | tf_op jit(solution)/shard_map/ppermute | solution.py:22
  14.0 3.2 %copy-start.7 = (s32[16]{0:T(128)S(1)}, s32[16]{0:T(128)}, u32[]{:S(2)}) copy-start(s32[16]{0:T(128)} %param.13) | copy-start | bytes 196
  14.0 3.4 %copy-start.6 = (s32[8,8,128]{2,1,0:T(8,128)S(1)}, s32[8,8,128]{2,1,0:T(8,128)}, u32[]{:S(2)}) copy-start(s32[8,8,128]{2,1,0:T(8,128)} %param.12) | copy-start | bytes 98308
  14.0 3.4 %copy-start.2 = (bf16[5,5,8,8,128]{4,3,2,1,0:T(8,128)(2,1)S(1)}, bf16[5,5,8,8,128]{4,3,2,1,0:T(8,128)(2,1)}, u32[]{:S(2)}) copy-start(bf16[5,5,8,8,128]{4,3,2,1,0:T(8,128)(2,1)} %param.9) | copy-start | bytes 1228804
  14.0 11.6 %collective-permute-start = (f32[5,8,1,128]{3,2,1,0:T(1,128)S(1)}, f32[5,8,1,128]{3,2,1,0:T(1,128)S(1)}, u32[]{:S(2)}, u32[]{:S(2)}) collective-permute-start(f32[5,8,1,128]{3,2,1,0:T(1,128)S(1)} %get-tuple-element.31), channel_id=1, source_target_pairs={{0,16},{16,32},{32,48},{48,64},{64,80},{80,96},{96,112},{112,128},... | collective-permute-start | bytes 61448 | tf_op jit(solution)/shard_map/ppermute | solution.py:20
  16.1 1.3 copy-start.5
  17.3 0.9 copy-start
  18.3 22.1 %copy-start.4 = (f32[5,8,8,128]{3,2,1,0:T(8,128)S(1)}, f32[5,8,8,128]{3,2,1,0:T(8,128)}, u32[]{:S(2)}) copy-start(f32[5,8,8,128]{3,2,1,0:T(8,128)} %param.8) | copy-start | bytes 491524
  25.6 13.7 %collective-permute-start.2 = (f32[5,1,10,128]{3,2,1,0:T(8,128)S(1)}, f32[5,1,10,128]{3,2,1,0:T(8,128)S(1)}, u32[]{:S(2)}, u32[]{:S(2)}) collective-permute-start(f32[5,1,10,128]{3,2,1,0:T(8,128)S(1)} %get-tuple-element.10), channel_id=1, source_target_pairs={{1,0},{2,1},{3,2},{4,3},{5,4},{6,5},{7,6},{8,7},{9,8},{10,9},{11,1... | collective-permute-start | bytes 76808 | tf_op jit(solution)/shard_map/ppermute | solution.py:22
  29.7 10.7 %collective-permute-start.3 = (f32[5,1,10,128]{3,2,1,0:T(8,128)S(1)}, f32[5,1,10,128]{3,2,1,0:T(8,128)S(1)}, u32[]{:S(2)}, u32[]{:S(2)}) collective-permute-start(f32[5,1,10,128]{3,2,1,0:T(8,128)S(1)} %get-tuple-element.11), channel_id=1, source_target_pairs={{0,1},{1,2},{2,3},{3,4},{4,5},{5,6},{6,7},{7,8},{8,9},{9,10},{10,1... | collective-permute-start | bytes 76808 | tf_op jit(solution)/shard_map/ppermute | solution.py:20
  40.4 1.0 copy-start.3
  41.8 5.4 %collective-permute-start.5 = (f32[5,8,1,128]{3,2,1,0:T(1,128)S(1)}, f32[5,8,1,128]{3,2,1,0:T(1,128)S(1)}, u32[]{:S(2)}, u32[]{:S(2)}) collective-permute-start(f32[5,8,1,128]{3,2,1,0:T(1,128)S(1)} %get-tuple-element.26), channel_id=1, source_target_pairs={{16,0},{32,16},{48,32},{64,48},{80,64},{96,80},{112,96},{128,112},... | collective-permute-start | bytes 61448 | tf_op jit(solution)/shard_map/ppermute | solution.py:22
  43.7 11.5 %collective-permute-start.4 = (f32[5,8,1,128]{3,2,1,0:T(1,128)S(1)}, f32[5,8,1,128]{3,2,1,0:T(1,128)S(1)}, u32[]{:S(2)}, u32[]{:S(2)}) collective-permute-start(f32[5,8,1,128]{3,2,1,0:T(1,128)S(1)} %get-tuple-element.27), channel_id=1, source_target_pairs={{0,16},{16,32},{32,48},{48,64},{64,80},{80,96},{96,112},{112,128},... | collective-permute-start | bytes 61448 | tf_op jit(solution)/shard_map/ppermute | solution.py:20
  55.2 14.2 %collective-permute-start.6 = (f32[5,1,10,128]{3,2,1,0:T(8,128)S(1)}, f32[5,1,10,128]{3,2,1,0:T(8,128)S(1)}, u32[]{:S(2)}, u32[]{:S(2)}) collective-permute-start(f32[5,1,10,128]{3,2,1,0:T(8,128)S(1)} %get-tuple-element.8), channel_id=1, source_target_pairs={{1,0},{2,1},{3,2},{4,3},{5,4},{6,5},{7,6},{8,7},{9,8},{10,9},{11,1... | collective-permute-start | bytes 76808 | tf_op jit(solution)/shard_map/ppermute | solution.py:22
  57.1 13.3 %collective-permute-start.7 = (f32[5,1,10,128]{3,2,1,0:T(8,128)S(1)}, f32[5,1,10,128]{3,2,1,0:T(8,128)S(1)}, u32[]{:S(2)}, u32[]{:S(2)}) collective-permute-start(f32[5,1,10,128]{3,2,1,0:T(8,128)S(1)} %get-tuple-element.9), channel_id=1, source_target_pairs={{0,1},{1,2},{2,3},{3,4},{4,5},{5,6},{6,7},{7,8},{8,9},{9,10},{10,1... | collective-permute-start | bytes 76808 | tf_op jit(solution)/shard_map/ppermute | solution.py:20
  70.9 5.4 %collective-permute-start.9 = (f32[5,8,1,128]{3,2,1,0:T(1,128)S(1)}, f32[5,8,1,128]{3,2,1,0:T(1,128)S(1)}, u32[]{:S(2)}, u32[]{:S(2)}) collective-permute-start(f32[5,8,1,128]{3,2,1,0:T(1,128)S(1)} %get-tuple-element.22), channel_id=1, source_target_pairs={{16,0},{32,16},{48,32},{64,48},{80,64},{96,80},{112,96},{128,112},... | collective-permute-start | bytes 61448 | tf_op jit(solution)/shard_map/ppermute | solution.py:22
  72.8 11.4 %collective-permute-start.8 = (f32[5,8,1,128]{3,2,1,0:T(1,128)S(1)}, f32[5,8,1,128]{3,2,1,0:T(1,128)S(1)}, u32[]{:S(2)}, u32[]{:S(2)}) collective-permute-start(f32[5,8,1,128]{3,2,1,0:T(1,128)S(1)} %get-tuple-element.23), channel_id=1, source_target_pairs={{0,16},{16,32},{32,48},{48,64},{64,80},{80,96},{96,112},{112,128},... | collective-permute-start | bytes 61448 | tf_op jit(solution)/shard_map/ppermute | solution.py:20
  84.3 13.7 %collective-permute-start.10 = (f32[5,1,10,128]{3,2,1,0:T(8,128)S(1)}, f32[5,1,10,128]{3,2,1,0:T(8,128)S(1)}, u32[]{:S(2)}, u32[]{:S(2)}) collective-permute-start(f32[5,1,10,128]{3,2,1,0:T(8,128)S(1)} %get-tuple-element.6), channel_id=1, source_target_pairs={{1,0},{2,1},{3,2},{4,3},{5,4},{6,5},{7,6},{8,7},{9,8},{10,9},{11,1... | collective-permute-start | bytes 76808 | tf_op jit(solution)/shard_map/ppermute | solution.py:22
  86.2 12.8 %collective-permute-start.11 = (f32[5,1,10,128]{3,2,1,0:T(8,128)S(1)}, f32[5,1,10,128]{3,2,1,0:T(8,128)S(1)}, u32[]{:S(2)}, u32[]{:S(2)}) collective-permute-start(f32[5,1,10,128]{3,2,1,0:T(8,128)S(1)} %get-tuple-element.7), channel_id=1, source_target_pairs={{0,1},{1,2},{2,3},{3,4},{4,5},{5,6},{6,7},{7,8},{8,9},{9,10},{10,1... | collective-permute-start | bytes 76808 | tf_op jit(solution)/shard_map/ppermute | solution.py:20
  99.5 5.4 %collective-permute-start.13 = (f32[5,8,1,128]{3,2,1,0:T(1,128)S(1)}, f32[5,8,1,128]{3,2,1,0:T(1,128)S(1)}, u32[]{:S(2)}, u32[]{:S(2)}) collective-permute-start(f32[5,8,1,128]{3,2,1,0:T(1,128)S(1)} %get-tuple-element.18), channel_id=1, source_target_pairs={{16,0},{32,16},{48,32},{64,48},{80,64},{96,80},{112,96},{128,112},... | collective-permute-start | bytes 61448 | tf_op jit(solution)/shard_map/ppermute | solution.py:22
  101.4 11.4 %collective-permute-start.12 = (f32[5,8,1,128]{3,2,1,0:T(1,128)S(1)}, f32[5,8,1,128]{3,2,1,0:T(1,128)S(1)}, u32[]{:S(2)}, u32[]{:S(2)}) collective-permute-start(f32[5,8,1,128]{3,2,1,0:T(1,128)S(1)} %get-tuple-element.19), channel_id=1, source_target_pairs={{0,16},{16,32},{32,48},{48,64},{64,80},{80,96},{96,112},{112,128},... | collective-permute-start | bytes 61448 | tf_op jit(solution)/shard_map/ppermute | solution.py:20
  112.9 13.7 %collective-permute-start.14 = (f32[5,1,10,128]{3,2,1,0:T(8,128)S(1)}, f32[5,1,10,128]{3,2,1,0:T(8,128)S(1)}, u32[]{:S(2)}, u32[]{:S(2)}) collective-permute-start(f32[5,1,10,128]{3,2,1,0:T(8,128)S(1)} %get-tuple-element.4), channel_id=1, source_target_pairs={{1,0},{2,1},{3,2},{4,3},{5,4},{6,5},{7,6},{8,7},{9,8},{10,9},{11,1... | collective-permute-start | bytes 76808 | tf_op jit(solution)/shard_map/ppermute | solution.py:22
  114.8 12.8 %collective-permute-start.15 = (f32[5,1,10,128]{3,2,1,0:T(8,128)S(1)}, f32[5,1,10,128]{3,2,1,0:T(8,128)S(1)}, u32[]{:S(2)}, u32[]{:S(2)}) collective-permute-start(f32[5,1,10,128]{3,2,1,0:T(8,128)S(1)} %get-tuple-element.5), channel_id=1, source_target_pairs={{0,1},{1,2},{2,3},{3,4},{4,5},{5,6},{6,7},{7,8},{8,9},{9,10},{10,1... | collective-permute-start | bytes 76808 | tf_op jit(solution)/shard_map/ppermute | solution.py:20
  128.0 28.3 %copy-start.1 = (f32[5,8,8,128]{3,2,1,0:T(8,128)}, f32[5,8,8,128]{3,2,1,0:T(8,128)S(1)}, u32[]{:S(2)}) copy-start(f32[5,8,8,128]{3,2,1,0:T(8,128)S(1)} %add_select_fusion) | copy-start | bytes 491524
  128.2 5.4 %collective-permute-start.17 = (f32[5,8,1,128]{3,2,1,0:T(1,128)S(1)}, f32[5,8,1,128]{3,2,1,0:T(1,128)S(1)}, u32[]{:S(2)}, u32[]{:S(2)}) collective-permute-start(f32[5,8,1,128]{3,2,1,0:T(1,128)S(1)} %get-tuple-element.14), channel_id=1, source_target_pairs={{16,0},{32,16},{48,32},{64,48},{80,64},{96,80},{112,96},{128,112},... | collective-permute-start | bytes 61448 | tf_op jit(solution)/shard_map/ppermute | solution.py:22
  130.1 11.5 %collective-permute-start.16 = (f32[5,8,1,128]{3,2,1,0:T(1,128)S(1)}, f32[5,8,1,128]{3,2,1,0:T(1,128)S(1)}, u32[]{:S(2)}, u32[]{:S(2)}) collective-permute-start(f32[5,8,1,128]{3,2,1,0:T(1,128)S(1)} %get-tuple-element.15), channel_id=1, source_target_pairs={{0,16},{16,32},{32,48},{48,64},{64,80},{80,96},{96,112},{112,128},... | collective-permute-start | bytes 61448 | tf_op jit(solution)/shard_map/ppermute | solution.py:20
  141.6 13.7 %collective-permute-start.18 = (f32[5,1,10,128]{3,2,1,0:T(8,128)S(1)}, f32[5,1,10,128]{3,2,1,0:T(8,128)S(1)}, u32[]{:S(2)}, u32[]{:S(2)}) collective-permute-start(f32[5,1,10,128]{3,2,1,0:T(8,128)S(1)} %get-tuple-element.2), channel_id=1, source_target_pairs={{1,0},{2,1},{3,2},{4,3},{5,4},{6,5},{7,6},{8,7},{9,8},{10,9},{11,1... | collective-permute-start | bytes 76808 | tf_op jit(solution)/shard_map/ppermute | solution.py:22
  143.5 12.8 %collective-permute-start.19 = (f32[5,1,10,128]{3,2,1,0:T(8,128)S(1)}, f32[5,1,10,128]{3,2,1,0:T(8,128)S(1)}, u32[]{:S(2)}, u32[]{:S(2)}) collective-permute-start(f32[5,1,10,128]{3,2,1,0:T(8,128)S(1)} %get-tuple-element.3), channel_id=1, source_target_pairs={{0,1},{1,2},{2,3},{3,4},{4,5},{5,6},{6,7},{7,8},{8,9},{9,10},{10,1... | collective-permute-start | bytes 76808 | tf_op jit(solution)/shard_map/ppermute | solution.py:20
  162.8 11.4 %collective-permute-start.20 = (f32[5,8,1,64]{3,2,1,0:T(1,128)S(1)}, f32[5,8,1,64]{3,2,1,0:T(1,128)S(1)}, u32[]{:S(2)}, u32[]{:S(2)}) collective-permute-start(f32[5,8,1,64]{3,2,1,0:T(1,128)S(1)} %slice.1103), channel_id=1, source_target_pairs={{0,16},{16,32},{32,48},{48,64},{64,80},{80,96},{96,112},{112,128},... | collective-permute-start | bytes 30728 | tf_op jit(solution)/shard_map/ppermute | solution.py:32
where the time goes:
time: 214 us; the launch traced here: 213 us
  starting transfers between devices  106 us (50%)
  waiting for transfers between devices  53.5 us (25%)
  blocking collectives  30.2 us (14%)
  local copies, waits for them, and re-layouts  18.4 us (9%)
  other arithmetic  3.49 us (2%)
    ppermute x10, starting transfers between devices, extended(): lax.ppermute(tail, axis, [(i, (i + 1) % count) for i in range(ends)])  72.4 us
    ppermute x10, waiting for transfers between devices, extended(): lax.ppermute(tail, axis, [(i, (i + 1) % count) for i in range(ends)])  44.4 us
    ppermute x10, starting transfers between devices, extended(): lax.ppermute(head, axis, [((i + 1) % count, i) for i in range(ends)])  31.7 us
    all_to_all x1, blocking collectives, shards(): lax.all_to_all(ordered, 'level', split_axis=0, concat_axis=0, tiled=True)  30.2 us
    ppermute x1, waiting for transfers between devices, passed_along(): return lax.ppermute(block, axis, route)  9.11 us
  transfers between devices with their start and end apart: 21, of which 11 were waited for; matrix products, arithmetic and copies ran while one was open for 1% of the time, Pallas kernels for 0%

commit v1 on v0

v1 whole, which is shorter than its diff:
```python
import jax
import jax.numpy as jnp
from jax import lax
from jax.sharding import PartitionSpec as P

SWEEPS = 4
relax_factor = 0.8
BOTH = ("brick", "level")


def far_pairs(count):
    return [(i, (i + 1) % count) for i in range(1, count, 2)]


def near_pairs(count):
    return [(i, i + 1) for i in range(0, count, 2)]


def split_wide(values):
    high = lax.reduce_precision(values, 8, 7)
    low = values - high
    return high.astype(jnp.bfloat16), low.astype(jnp.bfloat16)


def join_wide(high, low):
    return high.astype(jnp.float32) + low.astype(jnp.float32)


def matvec(rows, cells):
    count = cells.shape[0]
    fields = []
    for outer in range(count):
        total = rows(outer, 0) * cells[0]
        for inner in range(1, count):
            total = total + rows(outer, inner) * cells[inner]
        fields.append(total)
    return jnp.stack(fields)


def along_z(cells):
    zero = jnp.zeros_like(cells[..., :1])
    return jnp.concatenate([cells[..., 1:], zero], -1) + jnp.concatenate([zero, cells[..., :-1]], -1)


def operator(cells, neighbours, block, couple):
    diagonal = matvec(lambda outer, inner: block[inner, outer].astype(jnp.float32), cells)
    coupled = (
        couple[0] * neighbours[0] + couple[1] * neighbours[1] + couple[2] * along_z(cells)
    )
    return diagonal - coupled


def relaxed(cells, neighbours, block, precond, source, couple, keep):
    defect = source - operator(cells, neighbours, block, couple)
    step = matvec(lambda outer, inner: precond[outer, inner].astype(jnp.float32), defect)
    return jnp.where(keep, cells + relax_factor * step, 0.0)


def shards(adjoint, source, block, precond, couple, solid, coarse_owner):
    levels = lax.axis_size("level")
    bricks = lax.axis_size("brick")
    level = lax.axis_index("level")
    brick = lax.axis_index("brick")
    odd_l = level % 2 == 1
    odd_b = brick % 2 == 1
    fields = adjoint.shape[0]
    last = adjoint.shape[1] - 1
    keep = solid == 0

    f_valid = jnp.where(odd_l, level < levels - 1, level > 0)
    b_valid = jnp.where(odd_b, brick < bricks - 1, brick > 0)

    quads = [
        [b * levels + l for b in pair for l in side]
        for pair in far_pairs(bricks)
        for side in far_pairs(levels)
    ]
    a_groups = [list(pair) for pair in near_pairs(bricks)]
    n_groups = [list(pair) for pair in near_pairs(levels)]
    columns = [
        [b * levels + l for b in pair for l in range(levels)] for pair in far_pairs(bricks)
    ]

    def x_row(values, depth, above):
        low = values[..., depth, :, :]
        high = values[..., last - depth, :, :]
        return jnp.where(above, high, low)

    def y_row(values, depth, above):
        low = values[..., depth, :]
        high = values[..., last - depth, :]
        return jnp.where(above, high, low)

    edge_at = {
        "F": lambda v, d: x_row(v, d, odd_l),
        "N": lambda v, d: x_row(v, d, ~odd_l),
        "A": lambda v, d: y_row(v, d, ~odd_b),
        "B": lambda v, d: y_row(v, d, odd_b),
    }

    def facing(side, strip):
        above = {"F": odd_l, "N": ~odd_l, "A": ~odd_b, "B": odd_b}[side]
        return jnp.where(above, strip[..., last, :], strip[..., 0, :])

    def facing_back(side, strip):
        above = {"F": odd_l, "N": ~odd_l, "A": ~odd_b, "B": odd_b}[side]
        return jnp.where(above, strip[..., 0, :], strip[..., last, :])

    def state_planes(cells, side):
        both = jnp.concatenate([edge_at[side](cells, 0), edge_at[side](cells, 1)], 0)
        high, low = split_wide(both)
        return jnp.concatenate([high, low], 0)

    def fixed_planes(side):
        at = edge_at[side]
        order = (0, 1) if side in "FN" else (1, 0)
        pair = jnp.stack([couple[order[0]], couple[order[1]], couple[2]])
        wide = jnp.concatenate([at(source, 0), at(pair, 0)], 0)
        high, low = split_wide(wide)
        count = fields * fields
        return jnp.concatenate(
            [
                high,
                low,
                at(solid, 0)[None].astype(jnp.bfloat16),
                at(block, 0).reshape((count,) + high.shape[1:]),
                at(precond, 0).reshape((count,) + high.shape[1:]),
            ],
            0,
        )

    n_state = 4 * fields
    n_wide = fields + 3

    def corner_planes(corner):
        high, low = split_wide(corner)
        rows = last + 1
        return jnp.pad(jnp.stack([high, low]), ((0, 0), (0, rows - fields), (0, 0)))

    def corner_of(planes):
        return join_wide(planes[0, :fields], planes[1, :fields])

    def near_state(planes):
        return join_wide(planes[:fields], planes[2 * fields : 3 * fields])

    def deep_state(planes):
        return join_wide(planes[fields : 2 * fields], planes[3 * fields : 4 * fields])

    def exchange(cells, fixed):
        planes = {}
        for side in "FNAB":
            parts = [state_planes(cells, side)]
            if fixed is not None:
                parts.append(fixed[side])
            planes[side] = jnp.concatenate(parts, 0)
        to_even = jnp.where(odd_l, planes["F"], planes["B"])
        to_odd = jnp.where(odd_l, planes["B"], planes["F"])
        send = jnp.stack([to_odd, to_even, to_odd, to_even])
        got = lax.all_to_all(
            send, BOTH, split_axis=0, concat_axis=0, tiled=True, axis_index_groups=quads
        )
        mine = jnp.where(odd_b, got[:2], got[2:])
        other = jnp.where(odd_b, got[2:], got[:2])
        f_got = jnp.where(odd_l, mine[1], mine[0])
        b_got = jnp.where(odd_l, other[0], other[1])
        d_got = jnp.where(odd_l, other[1], other[0])
        zero = jnp.zeros((), jnp.float32)
        f_near = jnp.where(f_valid, near_state(f_got), zero)
        f_deep = jnp.where(f_valid, deep_state(f_got), zero)
        b_near = jnp.where(b_valid, near_state(b_got), zero)
        b_deep = jnp.where(b_valid, deep_state(b_got), zero)
        fb = jnp.where(f_valid & b_valid, facing_back("B", near_state(d_got)), zero)
        payload = jnp.concatenate([planes["A"], corner_planes(facing("A", f_near))], 0)
        got = lax.all_gather(payload, "brick", axis_index_groups=a_groups)
        a_got = jnp.where(odd_b, got[0], got[1])
        a_near, a_deep = near_state(a_got), deep_state(a_got)
        fa = corner_of(a_got[-2:])
        payload = jnp.concatenate(
            [
                planes["N"],
                corner_planes(facing("N", a_near)),
                corner_planes(facing("N", b_near)),
            ],
            0,
        )
        got = lax.all_gather(payload, "level", axis_index_groups=n_groups)
        n_got = jnp.where(odd_l, got[0], got[1])
        n_near, n_deep = near_state(n_got), deep_state(n_got)
        na = corner_of(n_got[-4:-2])
        nb = corner_of(n_got[-2:])

        strips = jnp.stack([f_near, n_near, a_near, b_near], 1)
        deep = jnp.stack([f_deep, n_deep, a_deep, b_deep], 1)
        low = jnp.stack(
            [
                jnp.where(odd_b, fa, fb),
                jnp.where(odd_b, na, nb),
                jnp.where(odd_l, na, fa),
                jnp.where(odd_l, nb, fb),
            ],
            1,
        )
        high = jnp.stack(
            [
                jnp.where(odd_b, fb, fa),
                jnp.where(odd_b, nb, na),
                jnp.where(odd_l, fa, na),
                jnp.where(odd_l, fb, nb),
            ],
            1,
        )
        received = {"F": f_got, "N": n_got, "A": a_got, "B": b_got}
        return strips, deep, low, high, received

    def around(strips):
        f, n, a, b = (strips[:, i] for i in range(4))
        x_low, x_high = jnp.where(odd_l, n, f), jnp.where(odd_l, f, n)
        y_low, y_high = jnp.where(odd_b, a, b), jnp.where(odd_b, b, a)
        return x_low, x_high, y_low, y_high

    def own_neighbours(cells, sides):
        x_low, x_high, y_low, y_high = sides
        tall = jnp.concatenate([x_low[:, None], cells, x_high[:, None]], 1)
        wide = jnp.concatenate([y_low[:, :, None], cells, y_high[:, :, None]], 2)
        return tall[:, 2:] + tall[:, :-2], wide[:, :, 2:] + wide[:, :, :-2]

    def inner_edges(cells):
        return jnp.stack([edge_at[side](cells, 0) for side in "FNAB"], 1)

    def strip_neighbours(cells, strips, deep, low, high):
        before = jnp.concatenate([low[:, :, None], strips[:, :, :-1]], 2)
        after = jnp.concatenate([strips[:, :, 1:], high[:, :, None]], 2)
        return deep + inner_edges(cells), before + after

    fixed = {side: fixed_planes(side) for side in "FNAB"}
    cells = adjoint
    ring = None
    for _ in range(SWEEPS // 2):
        strips, deep, low, high, received = exchange(cells, fixed if ring is None else None)
        if ring is None:
            wide = []
            masks = []
            blocks = []
            preconds = []
            for side in "FNAB":
                rest = received[side][n_state:]
                wide.append(join_wide(rest[:n_wide], rest[n_wide : 2 * n_wide]))
                open_cells = rest[2 * n_wide] == 0
                if side == "F":
                    open_cells = open_cells & f_valid
                if side == "B":
                    open_cells = open_cells & b_valid
                masks.append(open_cells)
                start = 2 * n_wide + 1
                count = fields * fields
                shape = (fields, fields) + rest.shape[1:]
                blocks.append(rest[start : start + count].reshape(shape))
                preconds.append(rest[start + count : start + 2 * count].reshape(shape))
            wide = jnp.stack(wide, 1)
            ring = {
                "source": wide[:fields],
                "couple": wide[fields:],
                "keep": jnp.stack(masks),
                "block": jnp.stack(blocks, 2),
                "precond": jnp.stack(preconds, 2),
            }
        first = relaxed(
            cells, own_neighbours(cells, around(strips)), block, precond, source, couple, keep
        )
        strips = relaxed(
            strips,
            strip_neighbours(cells, strips, deep, low, high),
            ring["block"],
            ring["precond"],
            ring["source"],
            ring["couple"],
            ring["keep"],
        )
        cells = relaxed(
            first, own_neighbours(first, around(strips)), block, precond, source, couple, keep
        )
    smoothed = cells

    nothing = jnp.zeros_like(strips)
    inside = own_neighbours(cells, around(nothing))
    residual = jnp.where(keep, source - operator(cells, inside, block, couple), 0.0)
    beyond = jnp.where(ring["keep"], ring["couple"][0] * inner_edges(cells), 0.0)
    x_low, x_high, y_low, y_high = around(beyond)

    def restrict(before, values, after, axis):
        length = values.shape[axis]
        even = lax.slice_in_dim(values, 0, length, 2, axis)
        odd = lax.slice_in_dim(values, 1, length, 2, axis)
        even = jnp.concatenate([jnp.zeros_like(before), even, after], axis)
        odd = jnp.concatenate([before, odd], axis)
        none = jnp.zeros_like(before)
        return (
            0.5 * even
            + 0.25 * jnp.concatenate([odd, none], axis)
            + 0.25 * jnp.concatenate([none, odd], axis)
        )

    along_x = restrict(x_low[:, None], residual, x_high[:, None], 1)
    blank = jnp.zeros_like(y_low[:, :1])
    y_low = restrict(blank, y_low, blank, 1)
    y_high = restrict(blank, y_high, blank, 1)
    both = restrict(y_low[:, :, None], along_x, y_high[:, :, None], 2)
    half_y = both.shape[2] - 2
    below, own, above = both[:, :, 0], both[:, :, 1:-1], both[:, :, -1]
    a_row = jnp.where(odd_b, below, above)
    b_row = jnp.where(odd_b, above, below)
    got = lax.all_gather(a_row, "brick", axis_index_groups=a_groups)
    a_got = jnp.where(odd_b, got[0], got[1])
    at_row = lax.broadcasted_iota(jnp.int32, (half_y, 1), 0)
    a_at = jnp.where(odd_b, 0, half_y - 1)
    own = own + jnp.where(at_row == a_at, a_got[:, :, None], 0.0)

    nz = adjoint.shape[3]
    zblock = nz // (2 * levels)
    slots = jnp.arange(levels, dtype=jnp.int32)
    inverse = jnp.sum(jnp.where(coarse_owner[None, :] == slots[:, None], slots[None, :], 0), axis=1)
    target = (inverse[:, None] * zblock + jnp.arange(zblock, dtype=jnp.int32)[None, :]).reshape(-1, 1)
    fine = jnp.arange(nz, dtype=jnp.int32)[None, :]
    weights = jnp.where(fine == 2 * target, 0.5, 0.0) + jnp.where(
        (fine == 2 * target + 1) | (fine == 2 * target - 1), 0.25, 0.0
    )

    def restrict_z(rows):
        flat = rows.reshape(-1, nz)
        flat = jnp.pad(flat, ((0, 128 - flat.shape[0]), (0, 0)))
        out = lax.dot_general(
            weights, flat, (((1,), (1,)), ((), ())), precision=lax.Precision.HIGHEST
        )
        return out.reshape(levels, zblock, 128)

    own_part = restrict_z(own)
    edge_part = restrict_z(b_row)
    send = jnp.where(
        odd_b,
        jnp.concatenate([own_part, edge_part], 0),
        jnp.concatenate([edge_part, own_part], 0),
    )
    got = lax.all_to_all(
        send, BOTH, split_axis=0, concat_axis=0, tiled=True, axis_index_groups=columns
    )
    own_got = jnp.where(odd_b, got[:levels], got[levels:])
    edge_got = jnp.where(odd_b, got[levels:], got[:levels])
    half_x = both.shape[1] - 2
    rows = fields * (half_x + 2)
    own_got = own_got[..., : rows * half_y].reshape(levels, zblock, fields, half_x + 2, half_y)
    edge_got = edge_got[..., :rows].reshape(levels, zblock, fields, half_x + 2, 1)
    b_at = jnp.where(odd_b, half_y - 1, 0)
    rest = jnp.where((jnp.arange(half_y) == b_at) & b_valid, edge_got, 0.0)
    total = own_got + rest
    up = total[:-1, :, :, -1:]
    down = total[1:, :, :, :1]
    none = jnp.zeros_like(total[:1, :, :, :1])
    up = jnp.concatenate([none, up], 0)
    down = jnp.concatenate([down, none], 0)
    body = total[:, :, :, 1:-1]
    body = jnp.concatenate(
        [body[:, :, :, :1] + up, body[:, :, :, 1:-1], body[:, :, :, -1:] + down], 3
    )
    coarse_rhs = body.transpose(2, 0, 3, 4, 1).reshape(
        fields, levels * half_x, half_y, zblock
    )[None]
    return (smoothed, coarse_rhs)


def solution(mesh):
    placed = (
        P(None, "level", "brick", None),
        P(None, "level", "brick", None),
        P(None, None, "level", "brick", None),
        P(None, None, "level", "brick", None),
        P(None, "level", "brick", None),
        P("level", "brick", None),
        P(),
    )
    return jax.shard_map(
        shards,
        mesh=mesh,
        in_specs=placed,
        out_specs=(P(None, "level", "brick", None), P("level", None, None, "brick", None)),
        check_vma=False,
    )
```

time: 214 us -> 124 us (0.58)
  the two profiles are of different devices: /device:TPU:33 before, /device:TPU:1 now
where the time goes in v1:
time: 124 us; the launch traced here: 123 us
  starting transfers between devices  47.6 us (38%)
  waiting for transfers between devices  30.4 us (25%)
  blocking collectives  23.7 us (19%)
  other arithmetic  9.07 us (7%)
  local copies, waits for them, and re-layouts  9.03 us (7%)
  between operations  2.63 us (2%)
    all_to_all x2, starting transfers between devices, exchange(): lax.all_to_all(send, BOTH, split_axis=0, concat_axis=0, tiled=True, axis_...  35.3 us
    all_to_all x2, waiting for transfers between devices, exchange(): lax.all_to_all(send, BOTH, split_axis=0, concat_axis=0, tiled=True, axis_...  23.5 us
    all_to_all x1, starting transfers between devices, shards(): lax.all_to_all(send, BOTH, split_axis=0, concat_axis=0, tiled=True, axis_...  12.2 us
    all_gather x2, blocking collectives, exchange(): got = lax.all_gather(payload, 'level', axis_index_groups=n_groups)  11.9 us
    all_gather x2, blocking collectives, exchange(): got = lax.all_gather(payload, 'brick', axis_index_groups=a_groups)  8.59 us
    all_to_all x1, waiting for transfers between devices, shards(): lax.all_to_all(send, BOTH, split_axis=0, concat_axis=0, tiled=True, axis_...  6.98 us
    all_gather x1, blocking collectives, shards(): got = lax.all_gather(a_row, 'brick', axis_index_groups=a_groups)  3.27 us
    unnamed x28, local copies, waits for them, and re-layouts  3.12 us
  transfers between devices with their start and end apart: 3, of which 3 were waited for; matrix products, arithmetic and copies ran while one was open for 1% of the time, Pallas kernels for 0%

profile of v1, /device:TPU:1, one launch (start us, length us, event | category | flops | bytes accessed | tf_op | source)
XLA Modules:
  0.0 123.0 jit_solution(12560594046161274439)
XLA Ops:
  0.7 0.9 slice_bitcast_fusion.55
  1.5 0.7 fusion.430
  2.3 1.4 %fusion.462 = (bf16[5,5,8,1,128]{4,3,2,1,0:T(2,128)(2,1)S(1)}, bf16[5,5,8,1,128]{4,3,2,1,0:T(2,128)(2,1)S(1)}) fusion(bf16[5,5,8,8,128]{4,3,2,1,0:T(8,128)(2,1)} %param.10), kind=kLoop, calls=%fused_computation.1229 | loop fusion | bytes 204800 | tf_op jit(solution)/shard_map/slice | solution.py:91
  3.6 0.9 bitcast_select_fusion
  4.6 0.1 fusion.463
  4.7 0.6 copy-done.4
  5.3 0.2 copy-done.3
  5.5 0.1 copy-done
  5.6 0.1 broadcast_select_fusion.24
  6.0 0.1 broadcast_select_fusion.10
  6.0 0.1 broadcast_select_fusion.5
  6.1 1.0 pad_maximum_fusion
  7.1 23.3 %all-to-all-start = ((bf16[4,87,8,128]{3,2,1,0:T(8,128)(2,1)}), bf16[4,87,8,128]{3,2,1,0:T(8,128)(2,1)S(1)}, u32[]{:S(2)}, u32[]{:S(2)}) async-start(bf16[4,87,8,128]{3,2,1,0:T(8,128)(2,1)} %pad_maximum_fusion), calls=%async_computation | async-start | bytes 1425408 | tf_op jit(solution)/shard_map/all_to_all | solution.py:159
  30.5 0.6 copy-done.5
  31.1 0.1 select_reduce_fusion
  31.3 0.1 add_multiply_fusion
  31.3 0.1 mul.1923
  31.9 0.1 fusion.474
  32.0 19.2 %all-to-all-done = bf16[4,87,8,128]{3,2,1,0:T(8,128)(2,1)S(1)} async-done(((bf16[4,87,8,128]{3,2,1,0:T(8,128)(2,1)}), bf16[4,87,8,128]{3,2,1,0:T(8,128)(2,1)S(1)}, u32[]{:S(2)}, u32[]{:S(2)}) %all-to-all-start) | async-done | bytes 712736 | tf_op jit(solution)/shard_map/all_to_all | solution.py:159
  51.2 0.1 broadcast_select_fusion.2
  51.4 0.1 slice_select_fusion.2
  51.6 5.0 %all-gather = bf16[178,8,128]{2,1,0:T(8,128)(2,1)S(1)} all-gather(bf16[89,8,128]{2,1,0:T(8,128)(2,1)S(1)} %constant_dynamic-update-slice_fusion.22), channel_id=2, replica_groups={{0,16},{32,48},{64,80},{96,112},{128,144},{160,176},{192,208},{224,240}..., dimensions={0}, use_global_device_ids=true | all-gather | bytes 546816 | tf_op jit(solution)/shard_map/all_gather | solution.py:174
  56.6 0.1 slice_select_fusion.1
  56.9 5.4 %all-gather.1 = bf16[182,8,128]{2,1,0:T(8,128)(2,1)S(1)} all-gather(bf16[91,8,128]{2,1,0:T(8,128)(2,1)S(1)} %constant_dynamic-update-slice_fusion.30), channel_id=3, replica_groups={{0,1},{2,3},{4,5},{6,7},{8,9},{10,11},{12,13},{14,15},{16,17},{18,19},{..., dimensions={0}, use_global_device_ids=true | all-gather | bytes 559104 | tf_op jit(solution)/shard_map/all_gather | solution.py:186
  62.4 0.1 fusion.484
  62.4 0.1 slice_select_fusion
  62.6 0.1 fusion.477
  62.8 0.1 fusion.38
  63.0 0.8 copy-done.2
  64.0 0.1 fusion.473
  64.6 0.1 fusion.61
  65.0 0.1 fusion.30
  65.3 0.1 broadcast_select_fusion.18
  65.5 0.7 pad_maximum_fusion.23
  66.2 12.0 %all-to-all-start.1 = ((bf16[4,20,8,128]{3,2,1,0:T(8,128)(2,1)}), bf16[4,20,8,128]{3,2,1,0:T(8,128)(2,1)S(1)}, u32[]{:S(2)}, u32[]{:S(2)}) async-start(bf16[4,20,8,128]{3,2,1,0:T(8,128)(2,1)} %pad_maximum_fusion.23), calls=%async_computation.1 | async-start | bytes 327680 | tf_op jit(solution)/shard_map/all_to_all | solution.py:159
  78.4 0.1 fusion.472
  78.5 4.3 %all-to-all-done.1 = bf16[4,20,8,128]{3,2,1,0:T(8,128)(2,1)S(1)} async-done(((bf16[4,20,8,128]{3,2,1,0:T(8,128)(2,1)}), bf16[4,20,8,128]{3,2,1,0:T(8,128)(2,1)S(1)}, u32[]{:S(2)}, u32[]{:S(2)}) %all-to-all-start.1) | async-done | bytes 163872 | tf_op jit(solution)/shard_map/all_to_all | solution.py:159
  82.9 3.6 %all-gather.2 = bf16[44,8,128]{2,1,0:T(8,128)(2,1)S(1)} all-gather(bf16[22,8,128]{2,1,0:T(8,128)(2,1)S(1)} %fusion.76), channel_id=4, replica_groups={{0,16},{32,48},{64,80},{96,112},{128,144},{160,176},{192,208},{224,240}..., dimensions={0}, use_global_device_ids=true | all-gather | bytes 135168 | tf_op jit(solution)/shard_map/all_gather | solution.py:174
  86.7 6.4 %all-gather.3 = bf16[48,8,128]{2,1,0:T(8,128)(2,1)S(1)} all-gather(bf16[24,8,128]{2,1,0:T(8,128)(2,1)S(1)} %fusion.75), channel_id=5, replica_groups={{0,1},{2,3},{4,5},{6,7},{8,9},{10,11},{12,13},{14,15},{16,17},{18,19},{..., dimensions={0}, use_global_device_ids=true | all-gather | bytes 147456 | tf_op jit(solution)/shard_map/all_gather | solution.py:186
  93.3 0.1 fusion.475
  93.4 0.1 fusion.22
  93.8 0.1 fusion.471
  94.2 0.1 fusion.67
  94.6 0.1 fusion.14
  95.2 0.1 fusion.470
  95.4 0.1 fusion.6
  95.6 0.2 slice.2243
  95.8 0.2 slice.2236
  96.1 0.1 fusion.44
  96.3 3.3 %all-gather.4 = f32[10,6,1,128]{3,2,1,0:T(1,128)S(1)} all-gather(f32[5,6,1,128]{3,2,1,0:T(1,128)S(1)} %copy.4569), channel_id=6, replica_groups={{0,16},{32,48},{64,80},{96,112},{128,144},{160,176},{192,208},{224,240}..., dimensions={0}, use_global_device_ids=true | all-gather | bytes 46080 | tf_op jit(solution)/shard_map/all_gather | solution.py:312
  99.6 0.1 slice_add_fusion
  99.7 0.3 fusion.72
  100.0 0.2 fusion.70
  100.2 0.6 maximum_select_fusion
  100.9 12.2 %all-to-all-start.2 = ((f32[32,4,128]{2,1,0:T(4,128)}), f32[32,4,128]{2,1,0:T(4,128)S(1)}, u32[]{:S(2)}, u32[]{:S(2)}) async-start(f32[32,4,128]{2,1,0:T(4,128)} %maximum_select_fusion), calls=%async_computation.2 | async-start | bytes 131072 | tf_op jit(solution)/shard_map/all_to_all | solution.py:343
  113.1 0.7 copy.4580
  113.8 7.0 %all-to-all-done.2 = f32[32,4,128]{2,1,0:T(4,128)S(1)} async-done(((f32[32,4,128]{2,1,0:T(4,128)}), f32[32,4,128]{2,1,0:T(4,128)S(1)}, u32[]{:S(2)}, u32[]{:S(2)}) %all-to-all-start.2) | async-done | bytes 65568 | tf_op jit(solution)/shard_map/all_to_all | solution.py:343
  120.8 0.1 copy.4577
  121.0 0.1 copy.4576
  121.1 0.1 select_add_fusion
  121.3 0.1 fusion.464
  121.3 0.1 slice_add_fusion.2
  121.5 0.5 copy.4579
  122.0 0.9 broadcast_in_dim_reshape.3
  (267 shorter events, 3.8 us)
Async XLA Ops:
  0.6 3.0 %copy-start.1 = (bf16[5,5,8,8,128]{4,3,2,1,0:T(8,128)(2,1)S(1)}, bf16[5,5,8,8,128]{4,3,2,1,0:T(8,128)(2,1)}, u32[]{:S(2)}) copy-start(bf16[5,5,8,8,128]{4,3,2,1,0:T(8,128)(2,1)} %param.9) | copy-start | bytes 1228804
  4.5 0.8 copy-start.4
  4.5 0.9 copy-start.3
  4.5 1.0 copy-start
  7.1 44.0 %all-to-all-start = ((bf16[4,87,8,128]{3,2,1,0:T(8,128)(2,1)}), bf16[4,87,8,128]{3,2,1,0:T(8,128)(2,1)S(1)}, u32[]{:S(2)}, u32[]{:S(2)}) async-start(bf16[4,87,8,128]{3,2,1,0:T(8,128)(2,1)} %pad_maximum_fusion), calls=%async_computation | async-start | bytes 1425408 | tf_op jit(solution)/shard_map/all_to_all | solution.py:159
  30.5 0.7 copy-start.5
  62.8 1.0 copy-start.2
  66.2 16.6 %all-to-all-start.1 = ((bf16[4,20,8,128]{3,2,1,0:T(8,128)(2,1)}), bf16[4,20,8,128]{3,2,1,0:T(8,128)(2,1)S(1)}, u32[]{:S(2)}, u32[]{:S(2)}) async-start(bf16[4,20,8,128]{3,2,1,0:T(8,128)(2,1)} %pad_maximum_fusion.23), calls=%async_computation.1 | async-start | bytes 327680 | tf_op jit(solution)/shard_map/all_to_all | solution.py:159
  100.9 19.9 %all-to-all-start.2 = ((f32[32,4,128]{2,1,0:T(4,128)}), f32[32,4,128]{2,1,0:T(4,128)S(1)}, u32[]{:S(2)}, u32[]{:S(2)}) async-start(f32[32,4,128]{2,1,0:T(4,128)} %maximum_select_fusion), calls=%async_computation.2 | async-start | bytes 131072 | tf_op jit(solution)/shard_map/all_to_all | solution.py:343

commit v2 on v1

--- a/solution.py
+++ b/solution.py
@@ -3,6 +3,7 @@
 from jax import lax
 from jax.sharding import PartitionSpec as P
 
+
 SWEEPS = 4
 relax_factor = 0.8
 BOTH = ("brick", "level")
@@ -14,6 +15,10 @@
 
 def near_pairs(count):
     return [(i, i + 1) for i in range(0, count, 2)]
+
+
+def both_ways(pairs):
+    return pairs + [(b, a) for a, b in pairs]
 
 
 def split_wide(values):
@@ -70,11 +75,8 @@
     f_valid = jnp.where(odd_l, level < levels - 1, level > 0)
     b_valid = jnp.where(odd_b, brick < bricks - 1, brick > 0)
 
-    quads = [
-        [b * levels + l for b in pair for l in side]
-        for pair in far_pairs(bricks)
-        for side in far_pairs(levels)
-    ]
+    b_route = both_ways(far_pairs(bricks)[:-1])
+    f_route = both_ways(far_pairs(levels)[:-1])
     a_groups = [list(pair) for pair in near_pairs(bricks)]
     n_groups = [list(pair) for pair in near_pairs(levels)]
     columns = [
@@ -101,10 +103,6 @@
     def facing(side, strip):
         above = {"F": odd_l, "N": ~odd_l, "A": ~odd_b, "B": odd_b}[side]
         return jnp.where(above, strip[..., last, :], strip[..., 0, :])
-
-    def facing_back(side, strip):
-        above = {"F": odd_l, "N": ~odd_l, "A": ~odd_b, "B": odd_b}[side]
-        return jnp.where(above, strip[..., 0, :], strip[..., last, :])
 
     def state_planes(cells, side):
         both = jnp.concatenate([edge_at[side](cells, 0), edge_at[side](cells, 1)], 0)
@@ -153,41 +151,25 @@
             if fixed is not None:
                 parts.append(fixed[side])
             planes[side] = jnp.concatenate(parts, 0)
-        to_even = jnp.where(odd_l, planes["F"], planes["B"])
-        to_odd = jnp.where(odd_l, planes["B"], planes["F"])
-        send = jnp.stack([to_odd, to_even, to_odd, to_even])
-        got = lax.all_to_all(
-            send, BOTH, split_axis=0, concat_axis=0, tiled=True, axis_index_groups=quads
-        )
-        mine = jnp.where(odd_b, got[:2], got[2:])
-        other = jnp.where(odd_b, got[2:], got[:2])
-        f_got = jnp.where(odd_l, mine[1], mine[0])
-        b_got = jnp.where(odd_l, other[0], other[1])
-        d_got = jnp.where(odd_l, other[1], other[0])
-        zero = jnp.zeros((), jnp.float32)
-        f_near = jnp.where(f_valid, near_state(f_got), zero)
-        f_deep = jnp.where(f_valid, deep_state(f_got), zero)
-        b_near = jnp.where(b_valid, near_state(b_got), zero)
-        b_deep = jnp.where(b_valid, deep_state(b_got), zero)
-        fb = jnp.where(f_valid & b_valid, facing_back("B", near_state(d_got)), zero)
-        payload = jnp.concatenate([planes["A"], corner_planes(facing("A", f_near))], 0)
-        got = lax.all_gather(payload, "brick", axis_index_groups=a_groups)
+
+        b_got = lax.ppermute(planes["B"], "brick", b_route)
+        got = lax.all_gather(planes["A"], "brick", axis_index_groups=a_groups)
         a_got = jnp.where(odd_b, got[0], got[1])
         a_near, a_deep = near_state(a_got), deep_state(a_got)
-        fa = corner_of(a_got[-2:])
-        payload = jnp.concatenate(
-            [
-                planes["N"],
-                corner_planes(facing("N", a_near)),
-                corner_planes(facing("N", b_near)),
-            ],
-            0,
-        )
-        got = lax.all_gather(payload, "level", axis_index_groups=n_groups)
+        b_near, b_deep = near_state(b_got), deep_state(b_got)
+
+        def with_ends(side):
+            ends = [corner_planes(facing(side, strip)) for strip in (a_near, b_near)]
+            return jnp.concatenate([planes[side]] + ends, 0)
+
+        f_send, n_send = with_ends("F"), with_ends("N")
+        f_got = lax.ppermute(f_send, "level", f_route)
+        got = lax.all_gather(n_send, "level", axis_index_groups=n_groups)
         n_got = jnp.where(odd_l, got[0], got[1])
+        f_near, f_deep = near_state(f_got), deep_state(f_got)
         n_near, n_deep = near_state(n_got), deep_state(n_got)
-        na = corner_of(n_got[-4:-2])
-        nb = corner_of(n_got[-2:])
+        fa, fb = corner_of(f_got[-4:-2]), corner_of(f_got[-2:])
+        na, nb = corner_of(n_got[-4:-2]), corner_of(n_got[-2:])
 
         strips = jnp.stack([f_near, n_near, a_near, b_near], 1)
         deep = jnp.stack([f_deep, n_deep, a_deep, b_deep], 1)

time: 124 us -> 120 us (0.968)
  the two profiles are of different devices: /device:TPU:1 before, /device:TPU:97 now
where the time goes in v2:
time: 120 us
  starting transfers between devices  41.5 us (35%)
  blocking collectives  31.9 us (27%)
  waiting for transfers between devices  29.3 us (24%)
  local copies, waits for them, and re-layouts  8.17 us (7%)
  other arithmetic  5.63 us (5%)
  between operations  2.62 us (2%)
    ppermute x2, starting transfers between devices, exchange(): f_got = lax.ppermute(f_send, 'level', f_route)  20.9 us
    all_gather x2, blocking collectives, exchange(): got = lax.all_gather(planes['A'], 'brick', axis_index_groups=a_groups)  18.8 us
    ppermute x2, waiting for transfers between devices, exchange(): f_got = lax.ppermute(f_send, 'level', f_route)  15.2 us
    all_to_all x1, starting transfers between devices, shards(): lax.all_to_all(send, BOTH, split_axis=0, concat_axis=0, tiled=True, axis_...  14.6 us
    all_to_all x1, waiting for transfers between devices, shards(): lax.all_to_all(send, BOTH, split_axis=0, concat_axis=0, tiled=True, axis_...  11.5 us
    all_gather x1, blocking collectives, shards(): got = lax.all_gather(a_row, 'brick', axis_index_groups=a_groups)  8.02 us
    ppermute x2, starting transfers between devices, exchange(): b_got = lax.ppermute(planes['B'], 'brick', b_route)  6.05 us
    all_gather x2, blocking collectives, exchange(): got = lax.all_gather(n_send, 'level', axis_index_groups=n_groups)  5.11 us
  transfers between devices with their start and end apart: 5, of which 4 were waited for; matrix products, arithmetic and copies ran while one was open for 2% of the time, Pallas kernels for 0%

profile of v2, /device:TPU:97, one launch (start us, length us, event | category | flops | bytes accessed | tf_op | source)
XLA Modules:
  0.0 119.6 jit_solution(11584381578234329679)
XLA Ops:
  0.7 1.0 copy.2060
  1.7 0.0 copy-start
  1.8 0.9 copy-done
  2.7 0.0 copy-start.5
  2.8 0.7 copy-done.5
  3.5 0.2 copy-done.2
  3.7 0.1 fusion.453
  3.8 0.1 fusion.454
  4.0 0.1 broadcast_select_fusion.2
  4.0 0.0 copy-start.3
  4.1 4.1 %collective-permute-start = (bf16[87,8,128]{2,1,0:T(8,128)(2,1)S(1)}, bf16[87,8,128]{2,1,0:T(8,128)(2,1)S(1)}, u32[]{:S(2)}, u32[]{:S(2)}) collective-permute-start(bf16[87,8,128]{2,1,0:T(8,128)(2,1)S(1)} %constant_dynamic-update-slice_fusion.15), channel_id=1, source_target_pairs={{16,32},{48,64},{80,96},{112,128},{144,160},{176,192},{208,224},{2... | collective-permute-start | bytes 534536 | tf_op jit(solution)/shard_map/ppermute | solution.py:155
  8.4 15.2 %all-gather = bf16[174,8,128]{2,1,0:T(8,128)(2,1)S(1)} all-gather(bf16[87,8,128]{2,1,0:T(8,128)(2,1)S(1)} %constant_dynamic-update-slice_fusion.8), channel_id=2, replica_groups={{0,16},{32,48},{64,80},{96,112},{128,144},{160,176},{192,208},{224,240}..., dimensions={0}, use_global_device_ids=true | all-gather | bytes 534528 | tf_op jit(solution)/shard_map/all_gather | solution.py:156
  23.6 0.1 fusion
  23.8 0.1 fusion.467
  24.3 0.6 copy-done.6
  24.9 0.1 select_reduce_fusion
  25.0 0.1 add_multiply_fusion
  25.1 0.1 mul.1923
  25.6 3.2 %all-gather.1 = bf16[182,8,128]{2,1,0:T(8,128)(2,1)S(1)} all-gather(bf16[91,8,128]{2,1,0:T(8,128)(2,1)S(1)} %constant_dynamic-update-slice_fusion.31), channel_id=3, replica_groups={{0,1},{2,3},{4,5},{6,7},{8,9},{10,11},{12,13},{14,15},{16,17},{18,19},{..., dimensions={0}, use_global_device_ids=true | all-gather | bytes 559104 | tf_op jit(solution)/shard_map/all_gather | solution.py:167
  28.8 0.1 fusion.478
  28.9 0.1 slice_select_fusion
  29.1 9.5 %collective-permute-start.1 = (bf16[91,8,128]{2,1,0:T(8,128)(2,1)S(1)}, bf16[91,8,128]{2,1,0:T(8,128)(2,1)S(1)}, u32[]{:S(2)}, u32[]{:S(2)}) collective-permute-start(bf16[91,8,128]{2,1,0:T(8,128)(2,1)S(1)} %constant_dynamic-update-slice_fusion.22), channel_id=1, source_target_pairs={{1,2},{3,4},{5,6},{7,8},{9,10},{11,12},{13,14},{2,1},{4,3},{6,5},{... | collective-permute-start | bytes 559112 | tf_op jit(solution)/shard_map/ppermute | solution.py:166
  38.6 13.5 %collective-permute-done.1 = bf16[91,8,128]{2,1,0:T(8,128)(2,1)S(1)} collective-permute-done((bf16[91,8,128]{2,1,0:T(8,128)(2,1)S(1)}, bf16[91,8,128]{2,1,0:T(8,128)(2,1)S(1)}, u32[]{:S(2)}, u32[]{:S(2)}) %collective-permute-start.1) | collective-permute-done | bytes 186400 | tf_op jit(solution)/shard_map/ppermute | solution.py:166
  52.1 0.1 fusion.472
  52.3 0.2 fusion.45
  52.7 0.1 fusion.466
  53.2 0.1 fusion.468
  53.7 0.2 fusion.37
  54.0 0.1 broadcast_select_fusion.19
  54.1 0.1 fusion.465
  54.3 3.5 %all-gather.2 = bf16[40,8,128]{2,1,0:T(8,128)(2,1)S(1)} all-gather(bf16[20,8,128]{2,1,0:T(8,128)(2,1)S(1)} %pad_maximum_fusion.41), channel_id=4, replica_groups={{0,16},{32,48},{64,80},{96,112},{128,144},{160,176},{192,208},{224,240}..., dimensions={0}, use_global_device_ids=true | all-gather | bytes 122880 | tf_op jit(solution)/shard_map/all_gather | solution.py:156
  57.9 1.9 %collective-permute-start.2 = (bf16[20,8,128]{2,1,0:T(8,128)(2,1)S(1)}, bf16[20,8,128]{2,1,0:T(8,128)(2,1)S(1)}, u32[]{:S(2)}, u32[]{:S(2)}) collective-permute-start(bf16[20,8,128]{2,1,0:T(8,128)(2,1)S(1)} %pad_maximum_fusion.43), channel_id=1, source_target_pairs={{16,32},{48,64},{80,96},{112,128},{144,160},{176,192},{208,224},{2... | collective-permute-start | bytes 122888 | tf_op jit(solution)/shard_map/ppermute | solution.py:155
  60.1 2.5 %collective-permute-done.2 = bf16[20,8,128]{2,1,0:T(8,128)(2,1)S(1)} collective-permute-done((bf16[20,8,128]{2,1,0:T(8,128)(2,1)S(1)}, bf16[20,8,128]{2,1,0:T(8,128)(2,1)S(1)}, u32[]{:S(2)}, u32[]{:S(2)}) %collective-permute-start.2) | collective-permute-done | bytes 40992 | tf_op jit(solution)/shard_map/ppermute | solution.py:155
  62.7 1.9 %all-gather.3 = bf16[48,8,128]{2,1,0:T(8,128)(2,1)S(1)} all-gather(bf16[24,8,128]{2,1,0:T(8,128)(2,1)S(1)} %fusion.77), channel_id=5, replica_groups={{0,1},{2,3},{4,5},{6,7},{8,9},{10,11},{12,13},{14,15},{16,17},{18,19},{..., dimensions={0}, use_global_device_ids=true | all-gather | bytes 147456 | tf_op jit(solution)/shard_map/all_gather | solution.py:167
  64.7 11.4 %collective-permute-start.3 = (bf16[24,8,128]{2,1,0:T(8,128)(2,1)S(1)}, bf16[24,8,128]{2,1,0:T(8,128)(2,1)S(1)}, u32[]{:S(2)}, u32[]{:S(2)}) collective-permute-start(bf16[24,8,128]{2,1,0:T(8,128)(2,1)S(1)} %fusion.75), channel_id=1, source_target_pairs={{1,2},{3,4},{5,6},{7,8},{9,10},{11,12},{13,14},{2,1},{4,3},{6,5},{... | collective-permute-start | bytes 147464 | tf_op jit(solution)/shard_map/ppermute | solution.py:166
  76.1 1.7 %collective-permute-done.3 = bf16[24,8,128]{2,1,0:T(8,128)(2,1)S(1)} collective-permute-done((bf16[24,8,128]{2,1,0:T(8,128)(2,1)S(1)}, bf16[24,8,128]{2,1,0:T(8,128)(2,1)S(1)}, u32[]{:S(2)}, u32[]{:S(2)}) %collective-permute-start.3) | collective-permute-done | bytes 49184 | tf_op jit(solution)/shard_map/ppermute | solution.py:166
  77.9 0.1 fusion.470
  78.1 0.2 fusion.29
  78.5 0.1 fusion.464
  78.8 0.1 fusion.65
  79.0 0.1 broadcast_select_fusion.14
  79.3 0.2 fusion.21
  79.6 0.1 fusion.463
  79.9 0.1 fusion.7
  80.0 0.2 slice.2124
  80.2 0.2 slice.2131
  80.6 0.1 fusion.66
  80.7 0.1 broadcast_select_fusion.12
  80.9 0.2 fusion.11
  81.3 8.0 %all-gather.4 = f32[10,6,1,128]{3,2,1,0:T(1,128)S(1)} all-gather(f32[5,6,1,128]{3,2,1,0:T(1,128)S(1)} %copy.2176), channel_id=6, replica_groups={{0,16},{32,48},{64,80},{96,112},{128,144},{160,176},{192,208},{224,240}..., dimensions={0}, use_global_device_ids=true | all-gather | bytes 46080 | tf_op jit(solution)/shard_map/all_gather | solution.py:294
  89.3 0.1 slice_add_fusion
  89.4 0.3 fusion.72
  89.7 0.2 fusion.70
  89.9 0.6 maximum_select_fusion
  90.6 14.6 %all-to-all-start = ((f32[32,4,128]{2,1,0:T(4,128)}), f32[32,4,128]{2,1,0:T(4,128)S(1)}, u32[]{:S(2)}, u32[]{:S(2)}) async-start(f32[32,4,128]{2,1,0:T(4,128)} %maximum_select_fusion), calls=%async_computation | async-start | bytes 131072 | tf_op jit(solution)/shard_map/all_to_all | solution.py:325
  105.2 0.7 copy.2184
  105.9 11.5 %all-to-all-done = f32[32,4,128]{2,1,0:T(4,128)S(1)} async-done(((f32[32,4,128]{2,1,0:T(4,128)}), f32[32,4,128]{2,1,0:T(4,128)S(1)}, u32[]{:S(2)}, u32[]{:S(2)}) %all-to-all-start) | async-done | bytes 65568 | tf_op jit(solution)/shard_map/all_to_all | solution.py:325
  117.5 0.1 copy.2181
  117.6 0.1 copy.2180
  117.7 0.1 select_add_fusion
  117.9 0.1 fusion.457
  118.0 0.1 slice_add_fusion.2
  118.1 0.5 copy.2183
  118.7 0.9 broadcast_in_dim_reshape.3
  (256 shorter events, 3.7 us)
Async XLA Ops:
  0.7 1.0 copy-start.4
  1.7 0.9 copy-start
  2.6 1.0 copy-start.2
  2.7 0.8 copy-start.5
  2.7 1.1 copy-start.1
  4.0 4.2 %copy-start.3 = (f32[5,8,8,128]{3,2,1,0:T(8,128)S(1)}, f32[5,8,8,128]{3,2,1,0:T(8,128)}, u32[]{:S(2)}) copy-start(f32[5,8,8,128]{3,2,1,0:T(8,128)} %param.7) | copy-start | bytes 491524
  4.1 21.4 %collective-permute-start = (bf16[87,8,128]{2,1,0:T(8,128)(2,1)S(1)}, bf16[87,8,128]{2,1,0:T(8,128)(2,1)S(1)}, u32[]{:S(2)}, u32[]{:S(2)}) collective-permute-start(bf16[87,8,128]{2,1,0:T(8,128)(2,1)S(1)} %constant_dynamic-update-slice_fusion.15), channel_id=1, source_target_pairs={{16,32},{48,64},{80,96},{112,128},{144,160},{176,192},{208,224},{2... | collective-permute-start | bytes 534536 | tf_op jit(solution)/shard_map/ppermute | solution.py:155
  24.2 0.7 copy-start.6
  29.1 23.0 %collective-permute-start.1 = (bf16[91,8,128]{2,1,0:T(8,128)(2,1)S(1)}, bf16[91,8,128]{2,1,0:T(8,128)(2,1)S(1)}, u32[]{:S(2)}, u32[]{:S(2)}) collective-permute-start(bf16[91,8,128]{2,1,0:T(8,128)(2,1)S(1)} %constant_dynamic-update-slice_fusion.22), channel_id=1, source_target_pairs={{1,2},{3,4},{5,6},{7,8},{9,10},{11,12},{13,14},{2,1},{4,3},{6,5},{... | collective-permute-start | bytes 559112 | tf_op jit(solution)/shard_map/ppermute | solution.py:166
  57.9 4.7 %collective-permute-start.2 = (bf16[20,8,128]{2,1,0:T(8,128)(2,1)S(1)}, bf16[20,8,128]{2,1,0:T(8,128)(2,1)S(1)}, u32[]{:S(2)}, u32[]{:S(2)}) collective-permute-start(bf16[20,8,128]{2,1,0:T(8,128)(2,1)S(1)} %pad_maximum_fusion.43), channel_id=1, source_target_pairs={{16,32},{48,64},{80,96},{112,128},{144,160},{176,192},{208,224},{2... | collective-permute-start | bytes 122888 | tf_op jit(solution)/shard_map/ppermute | solution.py:155
  64.7 13.2 %collective-permute-start.3 = (bf16[24,8,128]{2,1,0:T(8,128)(2,1)S(1)}, bf16[24,8,128]{2,1,0:T(8,128)(2,1)S(1)}, u32[]{:S(2)}, u32[]{:S(2)}) collective-permute-start(bf16[24,8,128]{2,1,0:T(8,128)(2,1)S(1)} %fusion.75), channel_id=1, source_target_pairs={{1,2},{3,4},{5,6},{7,8},{9,10},{11,12},{13,14},{2,1},{4,3},{6,5},{... | collective-permute-start | bytes 147464 | tf_op jit(solution)/shard_map/ppermute | solution.py:166
  90.6 26.9 %all-to-all-start = ((f32[32,4,128]{2,1,0:T(4,128)}), f32[32,4,128]{2,1,0:T(4,128)S(1)}, u32[]{:S(2)}, u32[]{:S(2)}) async-start(f32[32,4,128]{2,1,0:T(4,128)} %maximum_select_fusion), calls=%async_computation | async-start | bytes 131072 | tf_op jit(solution)/shard_map/all_to_all | solution.py:325

commit v3 on v2

--- a/solution.py
+++ b/solution.py
@@ -53,12 +53,6 @@
         couple[0] * neighbours[0] + couple[1] * neighbours[1] + couple[2] * along_z(cells)
     )
     return diagonal - coupled
-
-
-def relaxed(cells, neighbours, block, precond, source, couple, keep):
-    defect = source - operator(cells, neighbours, block, couple)
-    step = matvec(lambda outer, inner: precond[outer, inner].astype(jnp.float32), defect)
-    return jnp.where(keep, cells + relax_factor * step, 0.0)
 
 
 def shards(adjoint, source, block, precond, couple, solid, coarse_owner):
@@ -72,9 +66,7 @@
     last = adjoint.shape[1] - 1
     keep = solid == 0
 
-    f_valid = jnp.where(odd_l, level < levels - 1, level > 0)
     b_valid = jnp.where(odd_b, brick < bricks - 1, brick > 0)
-
     b_route = both_ways(far_pairs(bricks)[:-1])
     f_route = both_ways(far_pairs(levels)[:-1])
     a_groups = [list(pair) for pair in near_pairs(bricks)]
@@ -104,31 +96,12 @@
         above = {"F": odd_l, "N": ~odd_l, "A": ~odd_b, "B": odd_b}[side]
         return jnp.where(above, strip[..., last, :], strip[..., 0, :])
 
-    def state_planes(cells, side):
-        both = jnp.concatenate([edge_at[side](cells, 0), edge_at[side](cells, 1)], 0)
-        high, low = split_wide(both)
+    def planes_of(wide):
+        high, low = split_wide(wide)
         return jnp.concatenate([high, low], 0)
 
-    def fixed_planes(side):
-        at = edge_at[side]
-        order = (0, 1) if side in "FN" else (1, 0)
-        pair = jnp.stack([couple[order[0]], couple[order[1]], couple[2]])
-        wide = jnp.concatenate([at(source, 0), at(pair, 0)], 0)
-        high, low = split_wide(wide)
-        count = fields * fields
-        return jnp.concatenate(
-            [
-                high,
-                low,
-                at(solid, 0)[None].astype(jnp.bfloat16),
-                at(block, 0).reshape((count,) + high.shape[1:]),
-                at(precond, 0).reshape((count,) + high.shape[1:]),
-            ],
-            0,
-        )
-
-    n_state = 4 * fields
-    n_wide = fields + 3
+    def wide_of(planes, count):
+        return join_wide(planes[:count], planes[count : 2 * count])
 
     def corner_planes(corner):
         high, low = split_wide(corner)
@@ -138,61 +111,75 @@
     def corner_of(planes):
         return join_wide(planes[0, :fields], planes[1, :fields])
 
-    def near_state(planes):
-        return join_wide(planes[:fields], planes[2 * fields : 3 * fields])
-
-    def deep_state(planes):
-        return join_wide(planes[fields : 2 * fields], planes[3 * fields : 4 * fields])
-
-    def exchange(cells, fixed):
-        planes = {}
-        for side in "FNAB":
-            parts = [state_planes(cells, side)]
-            if fixed is not None:
-                parts.append(fixed[side])
-            planes[side] = jnp.concatenate(parts, 0)
-
-        b_got = lax.ppermute(planes["B"], "brick", b_route)
-        got = lax.all_gather(planes["A"], "brick", axis_index_groups=a_groups)
+    def preconditioned(precond, values):
+        return matvec(lambda outer, inner: precond[outer, inner].astype(jnp.float32), values)
+
+    open_couple = jnp.where(keep, couple, 0.0)
+    precond_edge = {side: edge_at[side](precond, 0) for side in "FNAB"}
+    keep_edge = {side: edge_at[side](keep, 0) for side in "FNAB"}
+
+    def fixed_planes(side):
+        at = edge_at[side]
+        order = (0, 1) if side in "FN" else (1, 0)
+        pair = jnp.stack([at(open_couple[axis], 0) for axis in order])
+        flat = precond_edge[side].reshape((fields * fields,) + pair.shape[1:])
+        return jnp.concatenate([planes_of(pair), flat], 0)
+
+    def state_planes(cells, defect, side):
+        edge = edge_at[side](cells, 0)
+        step = preconditioned(precond_edge[side], edge_at[side](defect, 0))
+        base = jnp.where(keep_edge[side], edge + relax_factor * step, 0.0)
+        return planes_of(jnp.concatenate([edge, base], 0))
+
+    n_state = 4 * fields
+    fixed_count = 4 + fields * fields
+    row_at = lax.broadcasted_iota(jnp.int32, (last + 1, 1), 0)
+
+    def across(low, high):
+        return jnp.where(row_at == 0, low, jnp.where(row_at == last, high, 0.0))
+
+    def exchange(cells, defect, fixed):
+        def planes(side, state):
+            return [state_planes(cells, state, side)] + ([fixed[side]] if fixed else [])
+
+        def opened(got):
+            wide = wide_of(got, 2 * fields)
+            return wide[:fields], wide[fields:], got[n_state : n_state + fixed_count]
+
+        b_send = jnp.concatenate(planes("B", defect), 0)
+        a_send = jnp.concatenate(planes("A", defect), 0)
+        b_got = lax.ppermute(b_send, "brick", b_route)
+        got = lax.all_gather(a_send, "brick", axis_index_groups=a_groups)
         a_got = jnp.where(odd_b, got[0], got[1])
-        a_near, a_deep = near_state(a_got), deep_state(a_got)
-        b_near, b_deep = near_state(b_got), deep_state(b_got)
+        a_near, a_base, a_fixed = opened(a_got)
+        b_near, b_base, b_fixed = opened(b_got)
+        y_low = jnp.where(odd_b, a_near, b_near)
+        y_high = jnp.where(odd_b, b_near, a_near)
+        defect = defect + couple[1] * across(y_low[:, :, None], y_high[:, :, None])
 
         def with_ends(side):
             ends = [corner_planes(facing(side, strip)) for strip in (a_near, b_near)]
-            return jnp.concatenate([planes[side]] + ends, 0)
+            return jnp.concatenate(planes(side, defect) + ends, 0)
 
         f_send, n_send = with_ends("F"), with_ends("N")
         f_got = lax.ppermute(f_send, "level", f_route)
         got = lax.all_gather(n_send, "level", axis_index_groups=n_groups)
         n_got = jnp.where(odd_l, got[0], got[1])
-        f_near, f_deep = near_state(f_got), deep_state(f_got)
-        n_near, n_deep = near_state(n_got), deep_state(n_got)
-        fa, fb = corner_of(f_got[-4:-2]), corner_of(f_got[-2:])
-        na, nb = corner_of(n_got[-4:-2]), corner_of(n_got[-2:])
-
-        strips = jnp.stack([f_near, n_near, a_near, b_near], 1)
-        deep = jnp.stack([f_deep, n_deep, a_deep, b_deep], 1)
-        low = jnp.stack(
-            [
-                jnp.where(odd_b, fa, fb),
-                jnp.where(odd_b, na, nb),
-                jnp.where(odd_l, na, fa),
-                jnp.where(odd_l, nb, fb),
-            ],
-            1,
-        )
-        high = jnp.stack(
-            [
-                jnp.where(odd_b, fb, fa),
-                jnp.where(odd_b, nb, na),
-                jnp.where(odd_l, fa, na),
-                jnp.where(odd_l, fb, nb),
-            ],
-            1,
-        )
-        received = {"F": f_got, "N": n_got, "A": a_got, "B": b_got}
-        return strips, deep, low, high, received
+        f_near, f_base, f_fixed = opened(f_got)
+        n_near, n_base, n_fixed = opened(n_got)
+        x_low = jnp.where(odd_l, n_near, f_near)[:, None]
+        x_high = jnp.where(odd_l, f_near, n_near)[:, None]
+        blank = jnp.zeros_like(cells[:, 2:])
+        defect = defect + couple[0] * jnp.concatenate([x_low, blank, x_high], 1)
+
+        none = jnp.zeros_like(f_near)
+        ends = [none, none]
+        for at in (-4, -2):
+            far, near = corner_of(f_got[at:][:2]), corner_of(n_got[at:][:2])
+            low, high = jnp.where(odd_l, near, far), jnp.where(odd_l, far, near)
+            ends.append(across(low[:, None], high[:, None]))
+        bases = jnp.stack([f_base, n_base, a_base, b_base], 1)
+        return defect, bases, jnp.stack(ends, 1), [f_fixed, n_fixed, a_fixed, b_fixed]
 
     def around(strips):
         f, n, a, b = (strips[:, i] for i in range(4))
@@ -209,64 +196,36 @@
     def inner_edges(cells):
         return jnp.stack([edge_at[side](cells, 0) for side in "FNAB"], 1)
 
-    def strip_neighbours(cells, strips, deep, low, high):
-        before = jnp.concatenate([low[:, :, None], strips[:, :, :-1]], 2)
-        after = jnp.concatenate([strips[:, :, 1:], high[:, :, None]], 2)
-        return deep + inner_edges(cells), before + after
-
-    fixed = {side: fixed_planes(side) for side in "FNAB"}
+    def defect_of(cells, strips):
+        return source - operator(cells, own_neighbours(cells, around(strips)), block, couple)
+
+    def relaxed(cells, defect):
+        step = preconditioned(precond, defect)
+        return jnp.where(keep, cells + relax_factor * step, 0.0)
+
     cells = adjoint
+    nothing = jnp.zeros((fields, 4) + adjoint.shape[2:], jnp.float32)
     ring = None
     for _ in range(SWEEPS // 2):
-        strips, deep, low, high, received = exchange(cells, fixed if ring is None else None)
+        fixed = None if ring else {side: fixed_planes(side) for side in "FNAB"}
+        defect = defect_of(cells, nothing)
+        defect, bases, ends, received = exchange(cells, defect, fixed)
         if ring is None:
-            wide = []
-            masks = []
-            blocks = []
-            preconds = []
-            for side in "FNAB":
-                rest = received[side][n_state:]
-                wide.append(join_wide(rest[:n_wide], rest[n_wide : 2 * n_wide]))
-                open_cells = rest[2 * n_wide] == 0
-                if side == "F":
-                    open_cells = open_cells & f_valid
-                if side == "B":
-                    open_cells = open_cells & b_valid
-                masks.append(open_cells)
-                start = 2 * n_wide + 1
-                count = fields * fields
-                shape = (fields, fields) + rest.shape[1:]
-                blocks.append(rest[start : start + count].reshape(shape))
-                preconds.append(rest[start + count : start + 2 * count].reshape(shape))
-            wide = jnp.stack(wide, 1)
+            pairs = jnp.stack([wide_of(got, 2) for got in received], 1)
+            shape = (fields, fields) + adjoint.shape[2:]
             ring = {
-                "source": wide[:fields],
-                "couple": wide[fields:],
-                "keep": jnp.stack(masks),
-                "block": jnp.stack(blocks, 2),
-                "precond": jnp.stack(preconds, 2),
+                "normal": pairs[0],
+                "tangent": pairs[1],
+                "precond": jnp.stack([got[4:].reshape(shape) for got in received], 2),
             }
-        first = relaxed(
-            cells, own_neighbours(cells, around(strips)), block, precond, source, couple, keep
-        )
-        strips = relaxed(
-            strips,
-            strip_neighbours(cells, strips, deep, low, high),
-            ring["block"],
-            ring["precond"],
-            ring["source"],
-            ring["couple"],
-            ring["keep"],
-        )
-        cells = relaxed(
-            first, own_neighbours(first, around(strips)), block, precond, source, couple, keep
-        )
+        first = relaxed(cells, defect)
+        missing = ring["normal"] * inner_edges(cells) + ring["tangent"] * ends
+        strips = bases + relax_factor * preconditioned(ring["precond"], missing)
+        cells = relaxed(first, defect_of(first, strips))
     smoothed = cells
 
-    nothing = jnp.zeros_like(strips)
-    inside = own_neighbours(cells, around(nothing))
-    residual = jnp.where(keep, source - operator(cells, inside, block, couple), 0.0)
-    beyond = jnp.where(ring["keep"], ring["couple"][0] * inner_edges(cells), 0.0)
+    residual = jnp.where(keep, defect_of(cells, nothing), 0.0)
+    beyond = ring["normal"] * inner_edges(cells)
     x_low, x_high, y_low, y_high = around(beyond)
 
     def restrict(before, values, after, axis):

time: 120 us -> 114 us (0.950)
  the two profiles are of different devices: /device:TPU:97 before, /device:TPU:41 now
where the time goes in v3:
time: 114 us
  starting transfers between devices  57.1 us (50%)
  waiting for transfers between devices  18.9 us (17%)
  blocking collectives  16.8 us (15%)
  local copies, waits for them, and re-layouts  11.2 us (10%)
  other arithmetic  6.21 us (5%)
  between operations  2.81 us (2%)
    ppermute x2, starting transfers between devices, exchange(): f_got = lax.ppermute(f_send, 'level', f_route)  20.4 us
    all_to_all x1, starting transfers between devices, shards(): lax.all_to_all(send, BOTH, split_axis=0, concat_axis=0, tiled=True, axis_...  19.6 us
    ppermute x2, starting transfers between devices, exchange(): b_got = lax.ppermute(b_send, 'brick', b_route)  17.2 us
    all_gather x2, blocking collectives, exchange(): got = lax.all_gather(a_send, 'brick', axis_index_groups=a_groups)  7.97 us
    ppermute x2, waiting for transfers between devices, exchange(): b_got = lax.ppermute(b_send, 'brick', b_route)  6.43 us
    all_to_all x1, waiting for transfers between devices, shards(): lax.all_to_all(send, BOTH, split_axis=0, concat_axis=0, tiled=True, axis_...  6.37 us
    ppermute x2, waiting for transfers between devices, exchange(): f_got = lax.ppermute(f_send, 'level', f_route)  6.09 us
    all_gather x2, blocking collectives, exchange(): got = lax.all_gather(n_send, 'level', axis_index_groups=n_groups)  5.59 us
  transfers between devices with their start and end apart: 5, of which 4 were waited for; matrix products, arithmetic and copies ran while one was open for 1% of the time, Pallas kernels for 0%

profile of v3, /device:TPU:41, one launch (start us, length us, event | category | flops | bytes accessed | tf_op | source)
XLA Modules:
  0.0 113.6 jit_solution(4793816377818386609)
XLA Ops:
  0.7 1.1 fusion.592
  1.7 0.9 copy.2268
  2.8 0.7 copy-done.8
  3.5 0.1 copy-done.6
  3.7 0.1 copy-done
  3.8 0.1 fusion.578
  3.9 0.1 fusion.593
  4.2 0.9 copy-done.1
  5.1 0.1 fusion.5
  5.5 13.2 %collective-permute-start = (bf16[49,8,128]{2,1,0:T(8,128)(2,1)S(1)}, bf16[49,8,128]{2,1,0:T(8,128)(2,1)S(1)}, u32[]{:S(2)}, u32[]{:S(2)}) collective-permute-start(bf16[49,8,128]{2,1,0:T(8,128)(2,1)S(1)} %constant_dynamic-update-slice_fusion.20), channel_id=1, source_target_pairs={{16,32},{48,64},{80,96},{112,128},{144,160},{176,192},{208,224},{2... | collective-permute-start | bytes 301064 | tf_op jit(solution)/shard_map/ppermute | solution.py:151
  19.0 4.2 %all-gather = bf16[98,8,128]{2,1,0:T(8,128)(2,1)S(1)} all-gather(bf16[49,8,128]{2,1,0:T(8,128)(2,1)S(1)} %constant_dynamic-update-slice_fusion.10), channel_id=2, replica_groups={{0,16},{32,48},{64,80},{96,112},{128,144},{160,176},{192,208},{224,240}..., dimensions={0}, use_global_device_ids=true | all-gather | bytes 301056 | tf_op jit(solution)/shard_map/all_gather | solution.py:152
  23.2 0.6 copy-done.5
  23.8 0.6 copy-done.9
  24.5 0.1 select_reduce_fusion
  24.6 0.1 pad.192.clone
  24.7 0.1 add_multiply_fusion
  24.8 0.1 mul.2933
  25.2 0.1 copy_add_fusion
  25.5 0.8 copy-done.2
  26.4 3.7 %all-gather.1 = bf16[106,8,128]{2,1,0:T(8,128)(2,1)S(1)} all-gather(bf16[53,8,128]{2,1,0:T(8,128)(2,1)S(1)} %constant_dynamic-update-slice_fusion.30), channel_id=3, replica_groups={{0,1},{2,3},{4,5},{6,7},{8,9},{10,11},{12,13},{14,15},{16,17},{18,19},{..., dimensions={0}, use_global_device_ids=true | all-gather | bytes 325632 | tf_op jit(solution)/shard_map/all_gather | solution.py:166
  30.4 10.2 %collective-permute-start.1 = (bf16[53,8,128]{2,1,0:T(8,128)(2,1)S(1)}, bf16[53,8,128]{2,1,0:T(8,128)(2,1)S(1)}, u32[]{:S(2)}, u32[]{:S(2)}) collective-permute-start(bf16[53,8,128]{2,1,0:T(8,128)(2,1)S(1)} %constant_dynamic-update-slice_fusion.42), channel_id=1, source_target_pairs={{1,2},{3,4},{5,6},{7,8},{9,10},{11,12},{13,14},{2,1},{4,3},{6,5},{... | collective-permute-start | bytes 325640 | tf_op jit(solution)/shard_map/ppermute | solution.py:165
  40.6 4.3 %collective-permute-done.1 = bf16[53,8,128]{2,1,0:T(8,128)(2,1)S(1)} collective-permute-done((bf16[53,8,128]{2,1,0:T(8,128)(2,1)S(1)}, bf16[53,8,128]{2,1,0:T(8,128)(2,1)S(1)}, u32[]{:S(2)}, u32[]{:S(2)}) %collective-permute-start.1) | collective-permute-done | bytes 108576 | tf_op jit(solution)/shard_map/ppermute | solution.py:165
  45.0 0.1 fusion.41
  45.3 0.1 fusion.590
  45.5 0.7 slice-done.2
  46.3 0.0 slice-done
  46.4 0.1 select_select_fusion.3
  46.5 0.1 fusion.57
  47.0 0.2 fusion.38
  47.4 0.1 fusion.588
  47.7 0.1 fusion.11
  48.2 3.8 %all-gather.2 = bf16[40,8,128]{2,1,0:T(8,128)(2,1)S(1)} all-gather(bf16[20,8,128]{2,1,0:T(8,128)(2,1)S(1)} %pad_maximum_fusion.27), channel_id=4, replica_groups={{0,16},{32,48},{64,80},{96,112},{128,144},{160,176},{192,208},{224,240}..., dimensions={0}, use_global_device_ids=true | all-gather | bytes 122880 | tf_op jit(solution)/shard_map/all_gather | solution.py:152
  52.1 3.9 %collective-permute-start.2 = (bf16[20,8,128]{2,1,0:T(8,128)(2,1)S(1)}, bf16[20,8,128]{2,1,0:T(8,128)(2,1)S(1)}, u32[]{:S(2)}, u32[]{:S(2)}) collective-permute-start(bf16[20,8,128]{2,1,0:T(8,128)(2,1)S(1)} %pad_maximum_fusion.29), channel_id=1, source_target_pairs={{16,32},{48,64},{80,96},{112,128},{144,160},{176,192},{208,224},{2... | collective-permute-start | bytes 122888 | tf_op jit(solution)/shard_map/ppermute | solution.py:151
  56.1 6.4 %collective-permute-done.2 = bf16[20,8,128]{2,1,0:T(8,128)(2,1)S(1)} collective-permute-done((bf16[20,8,128]{2,1,0:T(8,128)(2,1)S(1)}, bf16[20,8,128]{2,1,0:T(8,128)(2,1)S(1)}, u32[]{:S(2)}, u32[]{:S(2)}) %collective-permute-start.2) | collective-permute-done | bytes 40992 | tf_op jit(solution)/shard_map/ppermute | solution.py:151
  62.7 0.1 multiply_add_fusion.1
  63.1 1.9 %all-gather.3 = bf16[48,8,128]{2,1,0:T(8,128)(2,1)S(1)} all-gather(bf16[24,8,128]{2,1,0:T(8,128)(2,1)S(1)} %fusion.66), channel_id=5, replica_groups={{0,1},{2,3},{4,5},{6,7},{8,9},{10,11},{12,13},{14,15},{16,17},{18,19},{..., dimensions={0}, use_global_device_ids=true | all-gather | bytes 147456 | tf_op jit(solution)/shard_map/all_gather | solution.py:166
  65.1 10.2 %collective-permute-start.3 = (bf16[24,8,128]{2,1,0:T(8,128)(2,1)S(1)}, bf16[24,8,128]{2,1,0:T(8,128)(2,1)S(1)}, u32[]{:S(2)}, u32[]{:S(2)}) collective-permute-start(bf16[24,8,128]{2,1,0:T(8,128)(2,1)S(1)} %fusion.68), channel_id=1, source_target_pairs={{1,2},{3,4},{5,6},{7,8},{9,10},{11,12},{13,14},{2,1},{4,3},{6,5},{... | collective-permute-start | bytes 147464 | tf_op jit(solution)/shard_map/ppermute | solution.py:165
  75.4 1.7 %collective-permute-done.3 = bf16[24,8,128]{2,1,0:T(8,128)(2,1)S(1)} collective-permute-done((bf16[24,8,128]{2,1,0:T(8,128)(2,1)S(1)}, bf16[24,8,128]{2,1,0:T(8,128)(2,1)S(1)}, u32[]{:S(2)}, u32[]{:S(2)}) %collective-permute-start.3) | collective-permute-done | bytes 49184 | tf_op jit(solution)/shard_map/ppermute | solution.py:165
  77.1 0.1 select_select_fusion.1
  77.2 0.1 fusion.58
  77.4 0.1 fusion.42
  77.7 0.1 fusion.585
  77.8 0.1 stack.152
  78.3 0.2 fusion.30
  79.1 0.1 fusion.583
  79.2 0.1 fusion.18
  79.4 0.2 slice.2783
  79.6 0.2 slice.2776
  80.0 0.1 fusion.52
  80.1 3.3 %all-gather.4 = f32[10,6,1,128]{3,2,1,0:T(1,128)S(1)} all-gather(f32[5,6,1,128]{3,2,1,0:T(1,128)S(1)} %copy.2507), channel_id=6, replica_groups={{0,16},{32,48},{64,80},{96,112},{128,144},{160,176},{192,208},{224,240}..., dimensions={0}, use_global_device_ids=true | all-gather | bytes 46080 | tf_op jit(solution)/shard_map/all_gather | solution.py:253
  83.5 0.1 slice_add_fusion
  83.6 0.3 fusion.63
  83.9 0.2 fusion.61
  84.1 0.6 maximum_select_fusion
  84.7 19.6 %all-to-all-start = ((f32[32,4,128]{2,1,0:T(4,128)}), f32[32,4,128]{2,1,0:T(4,128)S(1)}, u32[]{:S(2)}, u32[]{:S(2)}) async-start(f32[32,4,128]{2,1,0:T(4,128)} %maximum_select_fusion), calls=%async_computation | async-start | bytes 131072 | tf_op jit(solution)/shard_map/all_to_all | solution.py:284
  104.3 0.7 copy.2518
  105.0 6.4 %all-to-all-done = f32[32,4,128]{2,1,0:T(4,128)S(1)} async-done(((f32[32,4,128]{2,1,0:T(4,128)}), f32[32,4,128]{2,1,0:T(4,128)S(1)}, u32[]{:S(2)}, u32[]{:S(2)}) %all-to-all-start) | async-done | bytes 65568 | tf_op jit(solution)/shard_map/all_to_all | solution.py:284
  111.4 0.1 copy.2515
  111.6 0.1 copy.2514
  111.7 0.1 select_add_fusion
  111.9 0.1 fusion.581
  112.0 0.1 slice_add_fusion.2
  112.1 0.5 copy.2517
  112.6 0.9 broadcast_in_dim_reshape.3
  (308 shorter events, 4.3 us)
Async XLA Ops:
  0.6 2.1 %copy-start.3 = (bf16[5,5,8,8,128]{4,3,2,1,0:T(8,128)(2,1)S(1)}, bf16[5,5,8,8,128]{4,3,2,1,0:T(8,128)(2,1)}, u32[]{:S(2)}) copy-start(bf16[5,5,8,8,128]{4,3,2,1,0:T(8,128)(2,1)} %param.9) | copy-start | bytes 1228804
  2.7 0.8 copy-start.8
  2.7 0.9 copy-start.6
  2.8 1.0 copy-start
  4.2 0.9 copy-start.1
  5.5 19.5 %collective-permute-start = (bf16[49,8,128]{2,1,0:T(8,128)(2,1)S(1)}, bf16[49,8,128]{2,1,0:T(8,128)(2,1)S(1)}, u32[]{:S(2)}, u32[]{:S(2)}) collective-permute-start(bf16[49,8,128]{2,1,0:T(8,128)(2,1)S(1)} %constant_dynamic-update-slice_fusion.20), channel_id=1, source_target_pairs={{16,32},{48,64},{80,96},{112,128},{144,160},{176,192},{208,224},{2... | collective-permute-start | bytes 301064 | tf_op jit(solution)/shard_map/ppermute | solution.py:151
  23.2 0.6 copy-start.5
  23.8 0.7 copy-start.9
  25.1 15.6 %copy-start.7 = (bf16[49,8,128]{2,1,0:T(8,128)(2,1)}, bf16[49,8,128]{2,1,0:T(8,128)(2,1)S(1)}, u32[]{:S(2)}) copy-start(bf16[49,8,128]{2,1,0:T(8,128)(2,1)S(1)} %collective-permute-done) | copy-start | bytes 301060
  25.4 0.9 copy-start.2
  30.1 10.5 %copy-start.4 = (bf16[1,53,8,128]{3,2,1,0:T(8,128)(2,1)}, bf16[1,53,8,128]{3,2,1,0:T(8,128)(2,1)S(1)}, u32[]{:S(2)}) copy-start(bf16[1,53,8,128]{3,2,1,0:T(8,128)(2,1)S(1)} %fusion.599) | copy-start | bytes 325636
  30.4 14.6 %collective-permute-start.1 = (bf16[53,8,128]{2,1,0:T(8,128)(2,1)S(1)}, bf16[53,8,128]{2,1,0:T(8,128)(2,1)S(1)}, u32[]{:S(2)}, u32[]{:S(2)}) collective-permute-start(bf16[53,8,128]{2,1,0:T(8,128)(2,1)S(1)} %constant_dynamic-update-slice_fusion.42), channel_id=1, source_target_pairs={{1,2},{3,4},{5,6},{7,8},{9,10},{11,12},{13,14},{2,1},{4,3},{6,5},{... | collective-permute-start | bytes 325640 | tf_op jit(solution)/shard_map/ppermute | solution.py:165
  45.5 0.8 slice-start.2
  45.5 0.8 slice-start
  45.5 0.8 slice-start.1
  52.1 10.5 %collective-permute-start.2 = (bf16[20,8,128]{2,1,0:T(8,128)(2,1)S(1)}, bf16[20,8,128]{2,1,0:T(8,128)(2,1)S(1)}, u32[]{:S(2)}, u32[]{:S(2)}) collective-permute-start(bf16[20,8,128]{2,1,0:T(8,128)(2,1)S(1)} %pad_maximum_fusion.29), channel_id=1, source_target_pairs={{16,32},{48,64},{80,96},{112,128},{144,160},{176,192},{208,224},{2... | collective-permute-start | bytes 122888 | tf_op jit(solution)/shard_map/ppermute | solution.py:151
  65.1 12.0 %collective-permute-start.3 = (bf16[24,8,128]{2,1,0:T(8,128)(2,1)S(1)}, bf16[24,8,128]{2,1,0:T(8,128)(2,1)S(1)}, u32[]{:S(2)}, u32[]{:S(2)}) collective-permute-start(bf16[24,8,128]{2,1,0:T(8,128)(2,1)S(1)} %fusion.68), channel_id=1, source_target_pairs={{1,2},{3,4},{5,6},{7,8},{9,10},{11,12},{13,14},{2,1},{4,3},{6,5},{... | collective-permute-start | bytes 147464 | tf_op jit(solution)/shard_map/ppermute | solution.py:165
  84.7 26.7 %all-to-all-start = ((f32[32,4,128]{2,1,0:T(4,128)}), f32[32,4,128]{2,1,0:T(4,128)S(1)}, u32[]{:S(2)}, u32[]{:S(2)}) async-start(f32[32,4,128]{2,1,0:T(4,128)} %maximum_select_fusion), calls=%async_computation | async-start | bytes 131072 | tf_op jit(solution)/shard_map/all_to_all | solution.py:284

commit v4 on v0

v4 whole, which is shorter than its diff:
```python
import functools

import jax
import jax.numpy as jnp
from jax import lax
from jax.experimental import pallas as pl
from jax.experimental.pallas import tpu as pltpu
from jax.sharding import PartitionSpec as P


relax_factor = 0.8
BOTH = ("brick", "level")
FIELDS = 5
SIDE = 8
TILE = SIDE * SIDE
LANES = 128
STATE = 4 * FIELDS
FIXED = 4 + FIELDS * FIELDS
HALF = SIDE // 2
OUTER = HALF + 2
f32 = jnp.float32


def far_pairs(count):
    return [(i, i + 1) for i in range(1, count - 1, 2)]


def near_pairs(count):
    return [[i, i + 1] for i in range(0, count, 2)]


def both_ways(pairs):
    return pairs + [(b, a) for a, b in pairs]


def iota(axis):
    return lax.broadcasted_iota(jnp.int32, (SIDE, LANES), axis)


def tile(ref, field, x):
    return ref[pl.ds((field * SIDE + x) * SIDE, SIDE), :]


def y_edge(ref, field, y):
    return ref[pl.ds(field * TILE + y, SIDE, stride=SIDE), :]


def put(ref, index, value):
    high = value.astype(jnp.bfloat16)
    ref[index] = high
    return (value - high.astype(f32)).astype(jnp.bfloat16)


def put_wide(ref, start, count, index, value):
    ref[start + count + index] = put(ref, start + index, value)


def wide(planes, start, count, index):
    return planes(start + index).astype(f32) + planes(start + count + index).astype(f32)


def shifted(value, axis):
    size = value.shape[axis]
    at = iota(axis)
    before = jnp.where(at == 0, 0.0, pltpu.roll(value, 1, axis))
    after = jnp.where(at == size - 1, 0.0, pltpu.roll(value, size - 1, axis))
    return before + after


def defect_tile(s, halo, source, block, couple, x):
    x_low, x_high, y_low, y_high = halo
    here = [tile(s, field, x) for field in range(FIELDS)]
    c0, c1, c2 = (tile(couple, axis, x) for axis in range(3))
    row = iota(0)
    out = []
    for outer in range(FIELDS):
        total = block[0, outer, x].astype(f32) * here[0]
        for inner in range(1, FIELDS):
            total = total + block[inner, outer, x].astype(f32) * here[inner]
        near_y = shifted(here[outer], 0)
        if y_low is not None:
            near_y = near_y + jnp.where(row == 0, y_low(outer, x), 0.0)
            near_y = near_y + jnp.where(row == SIDE - 1, y_high(outer, x), 0.0)
        coupled = c1 * near_y + c2 * shifted(here[outer], 1)
        near_x = None
        if x > 0:
            near_x = tile(s, outer, x - 1)
        elif x_low is not None:
            near_x = x_low(outer)
        other = None
        if x < SIDE - 1:
            other = tile(s, outer, x + 1)
        elif x_high is not None:
            other = x_high(outer)
        both = [v for v in (near_x, other) if v is not None]
        coupled = coupled + c0 * (both[0] if len(both) == 1 else both[0] + both[1])
        out.append(tile(source, outer, x) - (total - coupled))
    return out


def stepped(precond, defect):
    out = []
    for outer in range(FIELDS):
        total = precond(outer, 0) * defect[0]
        for inner in range(1, FIELDS):
            total = total + precond(outer, inner) * defect[inner]
        out.append(total)
    return out


def sweep(s, halo, ins, out):
    for x in range(SIDE):
        defect = defect_tile(s, halo, ins.source, ins.block, ins.couple, x)
        step = stepped(lambda o, i: ins.precond[o, i, x].astype(f32), defect)
        keep = ins.solid[pl.ds(x * SIDE, SIDE), :] == 0
        for field in range(FIELDS):
            value = jnp.where(keep, tile(s, field, x) + relax_factor * step[field], 0.0)
            out[pl.ds((field * SIDE + x) * SIDE, SIDE), :] = value


class Cells:
    def __init__(self, source, block, precond, couple, solid):
        self.source, self.block, self.precond = source, block, precond
        self.couple, self.solid = couple, solid


def y_state(s, ins, odd_b, sends, d, keeps, pf, opens):
    none = (None,) * 4
    for x in range(SIDE):
        defect = defect_tile(s, none, ins.source, ins.block, ins.couple, x)
        for field in range(FIELDS):
            d[pl.ds((field * SIDE + x) * SIDE, SIDE), :] = defect[field]
    for side, send in zip("BA", sends):
        above = odd_b if side == "B" else 1 - odd_b
        y = above * (SIDE - 1)
        p = [[y_edge(pf, o * FIELDS + i, y) for i in range(FIELDS)] for o in range(FIELDS)]
        step = stepped(lambda o, i: p[o][i], [y_edge(d, i, y) for i in range(FIELDS)])
        keep = y_edge(keeps, 0, y) == 0.0
        for field in range(FIELDS):
            edge = y_edge(s, field, y)
            put_wide(send, 0, 2 * FIELDS, field, edge)
            base = jnp.where(keep, edge + relax_factor * step[field], 0.0)
            put_wide(send, 0, 2 * FIELDS, FIELDS + field, base)
        if opens is not None:
            put_wide(send, STATE, 2, 0, y_edge(opens, 1, y))
            put_wide(send, STATE, 2, 1, y_edge(opens, 0, y))
            for o in range(FIELDS):
                for i in range(FIELDS):
                    send[STATE + 4 + o * FIELDS + i] = p[o][i].astype(jnp.bfloat16)


def fill(ins, pf, keeps, opens):
    for x in range(SIDE):
        solid = ins.solid[pl.ds(x * SIDE, SIDE), :]
        keeps[pl.ds(x * SIDE, SIDE), :] = solid.astype(f32)
        if opens is not None:
            for axis in range(2):
                rows = pl.ds((axis * SIDE + x) * SIDE, SIDE)
                opens[rows, :] = jnp.where(solid == 0, tile(ins.couple, axis, x), 0.0)
        for o in range(FIELDS):
            for i in range(FIELDS):
                rows = pl.ds(((o * FIELDS + i) * SIDE + x) * SIDE, SIDE)
                pf[rows, :] = ins.precond[o, i, x].astype(f32)


def first_kernel(
    odd, s_hbm, source_hbm, block_hbm, precond_hbm, couple_hbm, solid_hbm,
    s, source, block, precond, couple, solid, b_send, a_send,
    d, keeps, pf, opens, done,
):
    pairs = (
        (solid_hbm, solid), (couple_hbm, couple), (s_hbm, s),
        (precond_hbm, precond), (source_hbm, source), (block_hbm, block),
    )
    copies = [pltpu.make_async_copy(a, b, done.at[k]) for k, (a, b) in enumerate(pairs)]
    for copy in copies:
        copy.start()
    for copy in copies[:4]:
        copy.wait()
    ins = Cells(source, block, precond, couple, solid)
    fill(ins, pf, keeps, opens)
    for copy in copies[4:]:
        copy.wait()
    y_state(s, ins, odd[1], (b_send, a_send), d, keeps, pf, opens)


def y_halos(odd_b, b_got, a_got, low, high):
    partner = 1 - odd_b
    for field in range(FIELDS):
        a = wide(lambda k: a_got[partner, k], 0, 2 * FIELDS, field)
        b = wide(lambda k: b_got[k], 0, 2 * FIELDS, field)
        is_odd = odd_b == 1
        low[field] = jnp.where(is_odd, a, b)
        high[field] = jnp.where(is_odd, b, a)


def row_of(ref, field, x):
    return jnp.broadcast_to(ref[field, pl.ds(x, 1), :], (SIDE, LANES))


def second_kernel(
    fixed, odd, s, source, block, precond, couple, solid, b_got, a_got, f_send, n_send, low, high, flat
):
    ins = Cells(source, block, precond, couple, solid)
    odd_l, odd_b = odd[0], odd[1]
    is_odd = odd_l == 1
    y_halos(odd_b, b_got, a_got, low, high)
    halo = (None, None, lambda f, x: row_of(low, f, x), lambda f, x: row_of(high, f, x))
    ends = (0, SIDE - 1)
    edges, bases, pairs = [], [], []
    for x in ends:
        defect = defect_tile(s, halo, source, block, couple, x)
        step = stepped(lambda o, i: precond[o, i, x].astype(f32), defect)
        keep = solid[pl.ds(x * SIDE, SIDE), :] == 0
        edge = [tile(s, field, x) for field in range(FIELDS)]
        edges.append(edge)
        bases.append([jnp.where(keep, e + relax_factor * t, 0.0) for e, t in zip(edge, step)])
        pairs.append([jnp.where(keep, tile(couple, axis, x), 0.0) for axis in range(2)])
    for send, low_side in ((f_send, ~is_odd), (n_send, is_odd)):
        for field in range(FIELDS):
            put_wide(send, 0, 2 * FIELDS, field, jnp.where(low_side, edges[0][field], edges[1][field]))
            base = jnp.where(low_side, bases[0][field], bases[1][field])
            put_wide(send, 0, 2 * FIELDS, FIELDS + field, base)
        count = STATE
        if fixed:
            for axis in range(2):
                pair = jnp.where(low_side, pairs[0][axis], pairs[1][axis])
                put_wide(send, STATE, 2, axis, pair)
            for o in range(FIELDS):
                for i in range(FIELDS):
                    at_low = precond[o, i, 0].astype(f32)
                    at_high = precond[o, i, SIDE - 1].astype(f32)
                    value = jnp.where(low_side, at_low, at_high)
                    send[STATE + 4 + o * FIELDS + i] = value.astype(jnp.bfloat16)
            count += FIXED
        x = jnp.where(low_side, 0, SIDE - 1)
        for index, a_side in enumerate((True, False)):
            flat[...] = jnp.zeros((SIDE, LANES), f32)
            for field in range(FIELDS):
                at_low = low[field, pl.ds(x, 1), :]
                at_high = high[field, pl.ds(x, 1), :]
                low_is_it = (odd_b == 1) if a_side else (odd_b == 0)
                flat[pl.ds(field, 1), :] = jnp.where(low_is_it, at_low, at_high)
            put_wide(send, count + 2 * index, 1, 0, flat[...])


def ring_into(odd, s, got, fixed, low, high, x_low, x_high, corners):
    odd_l, odd_b = odd[0], odd[1]
    is_odd_l, is_odd_b = odd_l == 1, odd_b == 1
    row = iota(0)
    tail = STATE + (FIXED if got["fixed"] else 0)
    for k, (name, start) in enumerate((("F", tail), ("F", tail + 2), ("N", tail), ("N", tail + 2))):
        corners[k] = wide(got[name], start, 1, 0)
    rings = {}
    for side in "FNAB":
        planes, kept = got[side], fixed[side]
        normal = wide(kept, STATE, 2, 0)
        missing = []
        if side in "FN":
            above = odd_l if side == "F" else 1 - odd_l
            for field in range(FIELDS):
                inner = jnp.where(above == 1, tile(s, field, SIDE - 1), tile(s, field, 0))
                missing.append(normal * inner)
        else:
            above = odd_b if side == "B" else 1 - odd_b
            tangent = wide(kept, STATE, 2, 1)
            far, near = (0, 2) if side == "A" else (1, 3)
            for field in range(FIELDS):
                inner = y_edge(s, field, above * (SIDE - 1))
                far_row = row_of(corners, far, field)
                near_row = row_of(corners, near, field)
                first = jnp.where(is_odd_l, near_row, far_row)
                final = jnp.where(is_odd_l, far_row, near_row)
                ends = jnp.where(row == 0, first, jnp.where(row == SIDE - 1, final, 0.0))
                missing.append(normal * inner + tangent * ends)
        step = stepped(lambda o, i: kept(STATE + 4 + o * FIELDS + i).astype(f32), missing)
        rings[side] = [
            wide(planes, 0, 2 * FIELDS, FIELDS + field) + relax_factor * step[field]
            for field in range(FIELDS)
        ]
    for field in range(FIELDS):
        f, n, a, b = (rings[side][field] for side in "FNAB")
        x_low[field] = jnp.where(is_odd_l, n, f)
        x_high[field] = jnp.where(is_odd_l, f, n)
        low[field] = jnp.where(is_odd_b, a, b)
        high[field] = jnp.where(is_odd_b, b, a)


def two_sweeps(odd, s, ins, got, fixed, middle, out, halos):
    low, high, x_low, x_high, corners = halos
    odd_l, odd_b = odd[0], odd[1]
    is_odd_l = odd_l == 1
    y_halos(odd_b, *got["y"], low, high)
    for field in range(FIELDS):
        f = wide(got["F"], 0, 2 * FIELDS, field)
        n = wide(got["N"], 0, 2 * FIELDS, field)
        x_low[field] = jnp.where(is_odd_l, n, f)
        x_high[field] = jnp.where(is_odd_l, f, n)
    halo = (
        lambda field: x_low[field],
        lambda field: x_high[field],
        lambda field, x: row_of(low, field, x),
        lambda field, x: row_of(high, field, x),
    )
    sweep(s, halo, ins, middle)
    ring_into(odd, s, got, fixed, low, high, x_low, x_high, corners)
    sweep(middle, halo, ins, out)


def readers(odd, f_got, n_got, b_got, a_got):
    l, b = 1 - odd[0], 1 - odd[1]
    return {
        "F": lambda k: f_got[k],
        "N": lambda k: n_got[l, k],
        "A": lambda k: a_got[b, k],
        "B": lambda k: b_got[k],
    }


def third_kernel(
    odd, s, source, block, precond, couple, solid, f_got, n_got, b_got, a_got,
    out, b_send, a_send,
    middle, d, keeps, pf, low, high, x_low, x_high, corners,
):
    ins = Cells(source, block, precond, couple, solid)
    got = readers(odd, f_got, n_got, b_got, a_got)
    fixed = dict(got)
    got["fixed"], got["y"] = True, (b_got, a_got)
    two_sweeps(odd, s, ins, got, fixed, middle, out, (low, high, x_low, x_high, corners))
    fill(ins, pf, keeps, None)
    y_state(out, ins, odd[1], (b_send, a_send), d, keeps, pf, None)


def last_kernel(
    odd, s, source, block, precond, couple, solid, f_got, n_got, b_got, a_got, f_old, n_old, b_old, a_old,
    out, own, a_row, b_row,
    middle, low, high, x_low, x_high, corners, grid, below, above,
):
    ins = Cells(source, block, precond, couple, solid)
    got = readers(odd, f_got, n_got, b_got, a_got)
    fixed = readers(odd, f_old, n_old, b_old, a_old)
    got["fixed"], got["y"] = False, (b_got, a_got)
    two_sweeps(odd, s, ins, got, fixed, middle, out, (low, high, x_low, x_high, corners))
    odd_l, odd_b = odd[0], odd[1]
    is_odd_l, is_odd_b = odd_l == 1, odd_b == 1
    none = (None,) * 4
    for x in range(SIDE):
        defect = defect_tile(out, none, source, block, couple, x)
        keep = solid[pl.ds(x * SIDE, SIDE), :] == 0
        for field in range(FIELDS):
            rows = pl.ds((field * SIDE + x) * SIDE, SIDE)
            middle[rows, :] = jnp.where(keep, defect[field], 0.0)
    normal = {side: wide(fixed[side], STATE, 2, 0) for side in "FNAB"}
    row = iota(0)
    for field in range(FIELDS):
        y_at_a, y_at_b = (1 - odd_b) * (SIDE - 1), odd_b * (SIDE - 1)
        a = normal["A"] * y_edge(out, field, y_at_a)
        b = normal["B"] * y_edge(out, field, y_at_b)
        for ref, beyond in ((below, jnp.where(is_odd_b, a, b)), (above, jnp.where(is_odd_b, b, a))):
            even = 0.5 * beyond + 0.25 * shifted(beyond, 0)
            ref[pl.ds(field * OUTER, 1), :] = jnp.zeros((1, LANES), f32)
            for k in range(HALF):
                ref[pl.ds(field * OUTER + 1 + k, 1), :] = even[2 * k : 2 * k + 1]
            ref[pl.ds(field * OUTER + OUTER - 1, 1), :] = 0.25 * beyond[SIDE - 1 :]
    for field in range(FIELDS):
        first, final = tile(out, field, 0), tile(out, field, SIDE - 1)
        f = normal["F"] * jnp.where(is_odd_l, final, first)
        n = normal["N"] * jnp.where(is_odd_l, first, final)
        fine = [tile(middle, field, x) for x in range(SIDE)]
        before, after = jnp.where(is_odd_l, n, f), jnp.where(is_odd_l, f, n)
        coarse = [0.25 * before]
        for k in range(HALF):
            earlier = fine[2 * k - 1] if k else before
            coarse.append(0.5 * fine[2 * k] + 0.25 * (fine[2 * k + 1] + earlier))
        coarse.append(0.5 * after + 0.25 * fine[SIDE - 1])
        for k in range(OUTER):
            value = coarse[k]
            index = field * OUTER + k
            under = below[pl.ds(index, 1), :]
            even = 0.5 * value + 0.25 * shifted(value, 0)
            even = even + jnp.where(row == 0, jnp.broadcast_to(0.25 * under, (SIDE, LANES)), 0.0)
            grid[pl.ds(index * SIDE, SIDE), :] = even
            over = 0.5 * above[pl.ds(index, 1), :] + 0.25 * value[SIDE - 1 :]
            a_row[pl.ds(index, 1), :] = jnp.where(is_odd_b, 0.25 * under, over)
            b_row[pl.ds(index, 1), :] = jnp.where(is_odd_b, over, 0.25 * under)
    count = FIELDS * OUTER
    own[pl.ds(0, count * HALF), :] = grid[pl.ds(0, count * HALF, stride=2), :]
    own[pl.ds(count * HALF, LANES - count * HALF), :] = jnp.zeros((LANES - count * HALF, LANES), f32)
    b_row[pl.ds(count, LANES - count), :] = jnp.zeros((LANES - count, LANES), f32)
    a_row[pl.ds(count, 2), :] = jnp.zeros((2, LANES), f32)


def send_kernel(odd, weights, own, a_got, b_row, send, rows):
    odd_b = odd[1]
    count = FIELDS * OUTER
    rows[...] = own[...]
    at = pl.ds((1 - odd_b) * (HALF - 1), count, stride=HALF)
    rows[at, :] = rows[at, :] + a_got[1 - odd_b, pl.ds(0, count), :]

    values = jnp.concatenate([rows[...], b_row[...]], 0)
    size = weights.shape[0]
    total = jnp.zeros((size, 2 * LANES), f32)
    for _ in range(3):
        part = values.astype(jnp.bfloat16)
        values = values - part.astype(f32)
        total = total + lax.dot_general(
            weights[...], part, (((1,), (1,)), ((), ())), preferred_element_type=f32
        )
    send[pl.ds(pl.multiple_of((1 - odd_b) * size, size), size), :] = total[:, :LANES]
    send[pl.ds(pl.multiple_of(odd_b * size, size), size), :] = total[:, LANES:]


def call(kernel, outs, scratch, *args, resident=True):
    space = pltpu.VMEM if resident else pltpu.HBM
    args = [pltpu.with_memory_space_constraint(arg, space) for arg in args]
    copies = [] if resident else [pltpu.SemaphoreType.DMA((len(args),))]

    def body(*refs):
        kernel(tuple(lax.rem(lax.axis_index(axis), 2) for axis in ("level", "brick")), *refs)

    return pl.pallas_call(
        body,
        out_shape=[pltpu.VMEM(shape, dtype) for shape, dtype in outs],
        in_specs=[pl.BlockSpec(memory_space=space)] * len(args),
        out_specs=[pl.BlockSpec(memory_space=pltpu.VMEM)] * len(outs),
        scratch_shapes=[pltpu.VMEM(shape, f32) for shape in scratch] + copies,
        compiler_params=pltpu.CompilerParams(vmem_limit_bytes=16 * 1024 * 1024),
    )(*args)


def shards(adjoint, source, block, precond, couple, solid, coarse_owner):
    levels = lax.axis_size("level")
    bricks = lax.axis_size("brick")
    brick = lax.axis_index("brick")
    odd_b = brick % 2 == 1
    fields = adjoint.shape[0]

    b_valid = jnp.where(odd_b, brick < bricks - 1, brick > 0)
    b_route = both_ways(far_pairs(bricks))
    f_route = both_ways(far_pairs(levels))
    a_groups = near_pairs(bricks)
    n_groups = near_pairs(levels)
    columns = [
        [b * levels + l for b in pair for l in range(levels)]
        for pair in far_pairs(bricks) + [(bricks - 1, 0)]
    ]

    bf16 = jnp.bfloat16
    whole = ((FIELDS * TILE, LANES), f32)
    state = ((STATE, SIDE, LANES), bf16)
    full = ((STATE + FIXED, SIDE, LANES), bf16)
    state_ends = ((STATE + 4, SIDE, LANES), bf16)
    full_ends = ((STATE + FIXED + 4, SIDE, LANES), bf16)
    strip = (FIELDS, SIDE, LANES)
    corner = (4, SIDE, LANES)
    many = (FIELDS * FIELDS * TILE, LANES)

    flat = lambda values: values.reshape(-1, LANES)
    params = (flat(source), block, precond, flat(couple), flat(solid))
    cells = flat(adjoint)

    def brick_exchange(b_send, a_send):
        b_got = lax.ppermute(b_send, "brick", b_route)
        a_got = lax.all_gather(a_send, "brick", axis_index_groups=a_groups)
        return b_got, a_got

    def level_exchange(f_send, n_send):
        f_got = lax.ppermute(f_send, "level", f_route)
        n_got = lax.all_gather(n_send, "level", axis_index_groups=n_groups)
        return f_got, n_got

    given = (cells,) + params
    cells, *params, b_send, a_send = call(
        first_kernel, [(v.shape, v.dtype) for v in given] + [full, full],
        [whole[0], (TILE, LANES), many, (2 * TILE, LANES)], *given, resident=False,
    )
    b_got, a_got = brick_exchange(b_send, a_send)
    f_send, n_send = call(
        functools.partial(second_kernel, True), [full_ends, full_ends],
        [strip, strip, (SIDE, LANES)], cells, *params, b_got, a_got,
    )
    f_got, n_got = level_exchange(f_send, n_send)
    old = (f_got, n_got, b_got, a_got)
    cells, b_send, a_send = call(
        third_kernel, [whole, state, state],
        [whole[0], whole[0], (TILE, LANES), many, strip, strip, strip, strip, corner],
        cells, *params, *old,
    )
    b_got, a_got = brick_exchange(b_send, a_send)
    f_send, n_send = call(
        functools.partial(second_kernel, False), [state_ends, state_ends],
        [strip, strip, (SIDE, LANES)], cells, *params, b_got, a_got,
    )
    f_got, n_got = level_exchange(f_send, n_send)
    square = ((LANES, LANES), f32)
    smoothed, own, a_row, b_row = call(
        last_kernel, [whole, square, ((FIELDS * OUTER + 2, LANES), f32), square],
        [whole[0], strip, strip, strip, strip, corner, (FIELDS * OUTER * SIDE, LANES),
         (FIELDS * OUTER + 2, LANES), (FIELDS * OUTER + 2, LANES)],
        cells, *params, f_got, n_got, b_got, a_got, *old,
    )
    smoothed = smoothed.reshape(adjoint.shape)
    a_got = lax.all_gather(a_row, "brick", axis_index_groups=a_groups)
    half_x, half_y = HALF, HALF

    nz = adjoint.shape[3]
    zblock = nz // (2 * levels)
    slots = jnp.arange(levels, dtype=jnp.int32)
    inverse = jnp.sum(jnp.where(coarse_owner[None, :] == slots[:, None], slots[None, :], 0), axis=1)
    target = (inverse[:, None] * zblock + jnp.arange(zblock, dtype=jnp.int32)[None, :]).reshape(-1, 1)
    fine = jnp.arange(nz, dtype=jnp.int32)[None, :]
    weights = jnp.where(fine == 2 * target, 0.5, 0.0) + jnp.where(
        (fine == 2 * target + 1) | (fine == 2 * target - 1), 0.25, 0.0
    )

    (send,) = call(
        send_kernel, [square], [square[0]], weights.astype(bf16), own, a_got, b_row
    )
    send = send.reshape(2 * levels, zblock, LANES)
    got = lax.all_to_all(
        send, BOTH, split_axis=0, concat_axis=0, tiled=True, axis_index_groups=columns
    )
    own_got = jnp.where(odd_b, got[:levels], got[levels:])
    edge_got = jnp.where(odd_b, got[levels:], got[:levels])
    rows = fields * (half_x + 2)
    own_got = own_got[..., : rows * half_y].reshape(levels, zblock, fields, half_x + 2, half_y)
    edge_got = edge_got[..., :rows].reshape(levels, zblock, fields, half_x + 2, 1)
    b_at = jnp.where(odd_b, half_y - 1, 0)
    rest = jnp.where((jnp.arange(half_y) == b_at) & b_valid, edge_got, 0.0)
    total = own_got + rest
    up = total[:-1, :, :, -1:]
    down = total[1:, :, :, :1]
    none = jnp.zeros_like(total[:1, :, :, :1])
    up = jnp.concatenate([none, up], 0)
    down = jnp.concatenate([down, none], 0)
    body = total[:, :, :, 1:-1]
    body = jnp.concatenate(
        [body[:, :, :, :1] + up, body[:, :, :, 1:-1], body[:, :, :, -1:] + down], 3
    )
    coarse_rhs = body.transpose(2, 0, 3, 4, 1).reshape(
        fields, levels * half_x, half_y, zblock
    )[None]
    return (smoothed, coarse_rhs)


def solution(mesh):
    placed = (
        P(None, "level", "brick", None),
        P(None, "level", "brick", None),
        P(None, None, "level", "brick", None),
        P(None, None, "level", "brick", None),
        P(None, "level", "brick", None),
        P("level", "brick", None),
        P(),
    )
    return jax.shard_map(
        shards,
        mesh=mesh,
        in_specs=placed,
        out_specs=(P(None, "level", "brick", None), P("level", None, None, "brick", None)),
        check_vma=False,
    )
```

time: 214 us -> 93.6 us (0.44)
  waiting for transfers between devices: 53.5 us -> 6.78 us
  starting transfers between devices: 106 us -> 62.1 us
  local copies, waits for them, and re-layouts: 18.4 us -> 2.57 us
  blocking collectives: 30.2 us -> 15.6 us
  Pallas kernels: 0 us -> 4.78 us
  other arithmetic: 3.49 us -> 0.6 us
    ppermute x21 -> x4, starting transfers between devices: 106 us -> 43.7 us  [the longest x2 22.1 us: level_exchange(): f_got = lax.ppermute(f_send, 'level', f_route)]
    ppermute x21 -> x4, waiting for transfers between devices: 53.5 us -> 0.73 us  [the longest x2 0.73 us: level_exchange(): f_got = lax.ppermute(f_send, 'level', f_route)]
    all_to_all x1 -> x0, blocking collectives: 30.2 us -> none  [shards(): lax.all_to_all(ordered, 'level', split_axis=0, concat_axis=0, tiled=True)]
    all_to_all x0 -> x1, starting transfers between devices: none -> 18.4 us  [shards(): lax.all_to_all(send, BOTH, split_axis=0, concat_axis=0, tiled=True, axis_...]
    all_gather x0 -> x5, blocking collectives: none -> 15.6 us  [the longest x2 8.52 us: brick_exchange(): a_got = lax.all_gather(a_send, 'brick', axis_index_groups=a_groups)]
    slice x21 -> x5, local copies, waits for them, and re-layouts: 11.3 us -> 0.33 us  [the longest x1 0.12 us: shards(): own_got[..., :rows * half_y]]
    all_to_all x0 -> x1, waiting for transfers between devices: none -> 6.04 us  [shards(): lax.all_to_all(send, BOTH, split_axis=0, concat_axis=0, tiled=True, axis_...]
    pallas_call x0 -> x6, Pallas kernels: none -> 4.78 us  [call(): pl.pallas_call(body, out_shape=[pltpu.VMEM(shape, dtype) for shape, dtype...]
  transfers between devices with their start and end apart: 21 -> 5, of which waited for: 11 -> 3; matrix products, arithmetic and copies ran while one was open for 1% -> 1% of each run, Pallas kernels for 0% -> 0%
where the time goes in v4:
time: 93.6 us; the launch traced here: 93.2 us
  starting transfers between devices  62.1 us (66%)
  blocking collectives  15.6 us (17%)
  waiting for transfers between devices  6.78 us (7%)
  Pallas kernels  4.78 us (5%)
  local copies, waits for them, and re-layouts  2.57 us (3%)
    ppermute x2, starting transfers between devices, level_exchange(): f_got = lax.ppermute(f_send, 'level', f_route)  22.1 us
    ppermute x2, starting transfers between devices, brick_exchange(): b_got = lax.ppermute(b_send, 'brick', b_route)  21.6 us
    all_to_all x1, starting transfers between devices, shards(): lax.all_to_all(send, BOTH, split_axis=0, concat_axis=0, tiled=True, axis_...  18.4 us
    all_gather x2, blocking collectives, brick_exchange(): a_got = lax.all_gather(a_send, 'brick', axis_index_groups=a_groups)  8.52 us
    all_to_all x1, waiting for transfers between devices, shards(): lax.all_to_all(send, BOTH, split_axis=0, concat_axis=0, tiled=True, axis_...  6.04 us
    pallas_call x6, Pallas kernels, call(): pl.pallas_call(body, out_shape=[pltpu.VMEM(shape, dtype) for shape, dtype...  4.78 us
    all_gather x2, blocking collectives, level_exchange(): n_got = lax.all_gather(n_send, 'level', axis_index_groups=n_groups)  3.84 us
    all_gather x1, blocking collectives, shards(): a_got = lax.all_gather(a_row, 'brick', axis_index_groups=a_groups)  3.25 us
  transfers between devices with their start and end apart: 5, of which 3 were waited for; matrix products, arithmetic and copies ran while one was open for 1% of the time, Pallas kernels for 0%

profile of v4, /device:TPU:33, one launch (start us, length us, event | category | flops | bytes accessed | tf_op | source)
XLA Modules:
  0.0 93.2 jit_solution(16449768466666880042)
XLA Ops:
  0.6 1.6 %shard_map.86 = (f32[320,128]{1,0:T(8,128)S(1)}, f32[320,128]{1,0:T(8,128)S(1)}, bf16[5,5,8,8,128]{4,3,2,1,0:T(8,128)(2,1)S(1)}, bf16[5,5,8,8,128]{4,3,2,1,0:T(8...) custom-call(f32[320,128]{1,0:T(8,128)} %bitcast.31, ...), custom_call_target="tpu_custom_call" | custom-call | tf_op jit(solution)/shard_map/pallas_call | solution.py:421
  2.3 0.0 copy-start
  2.3 12.3 %collective-permute-start = (bf16[49,8,128]{2,1,0:T(8,128)(2,1)S(1)}, bf16[49,8,128]{2,1,0:T(8,128)(2,1)S(1)}, u32[]{:S(2)}, u32[]{:S(2)}) collective-permute-start(bf16[49,8,128]{2,1,0:T(8,128)(2,1)S(1)} %get-tuple-element.27), channel_id=1, source_target_pairs={{16,32},{48,64},{80,96},{112,128},{144,160},{176,192},{208,224},{2... | collective-permute-start | bytes 301064 | tf_op jit(solution)/shard_map/ppermute | solution.py:463
  14.6 0.0 copy-done
  14.6 0.1 select_reduce_fusion
  14.8 5.0 %all-gather = bf16[98,8,128]{2,1,0:T(8,128)(2,1)S(1)} all-gather(bf16[49,8,128]{2,1,0:T(8,128)(2,1)S(1)} %get-tuple-element.28), channel_id=2, replica_groups={{0,16},{32,48},{64,80},{96,112},{128,144},{160,176},{192,208},{224,240}..., dimensions={0}, use_global_device_ids=true | all-gather | bytes 301056 | tf_op jit(solution)/shard_map/all_gather | solution.py:464
  19.8 0.0 collective-permute-done.refs_6_.refs_8_.refs_12_
  19.8 0.1 shard_map.87
  19.9 12.4 %collective-permute-start.1 = (bf16[53,8,128]{2,1,0:T(8,128)(2,1)S(1)}, bf16[53,8,128]{2,1,0:T(8,128)(2,1)S(1)}, u32[]{:S(2)}, u32[]{:S(2)}) collective-permute-start(bf16[53,8,128]{2,1,0:T(8,128)(2,1)S(1)} %get-tuple-element.29), channel_id=1, source_target_pairs={{1,2},{3,4},{5,6},{7,8},{9,10},{11,12},{13,14},{2,1},{4,3},{6,5},{... | collective-permute-start | bytes 325640 | tf_op jit(solution)/shard_map/ppermute | solution.py:468
  32.3 0.1 add_multiply_fusion
  32.4 0.1 mul.29
  32.5 2.0 %all-gather.1 = bf16[106,8,128]{2,1,0:T(8,128)(2,1)S(1)} all-gather(bf16[53,8,128]{2,1,0:T(8,128)(2,1)S(1)} %get-tuple-element.30), channel_id=3, replica_groups={{0,1},{2,3},{4,5},{6,7},{8,9},{10,11},{12,13},{14,15},{16,17},{18,19},{..., dimensions={0}, use_global_device_ids=true | all-gather | bytes 325632 | tf_op jit(solution)/shard_map/all_gather | solution.py:469
  34.5 0.6 collective-permute-done.1.refs_6_.refs_10_
  35.0 1.0 %shard_map.88 = (f32[320,128]{1,0:T(8,128)S(1)}, bf16[20,8,128]{2,1,0:T(8,128)(2,1)S(1)}, bf16[20,8,128]{2,1,0:T(8,128)(2,1)S(1)}) custom-call(f32[320,128]{1,0:T(8,128)S(1)} %get-tuple-element.21.refs_0_, f32[320,128]{1,0:T(8,128)S(1)} %get-tuple-element.22.refs_1_, bf16[5,5,8,8,128]{4,3,2,1,0:T(8,128)(2,1)S(1)} %get-tuple-element.23.refs_2_, ...), custom_call_target="tpu_custom_call" | custom-call | tf_op jit(solution)/shard_map/pallas_call | solution.py:421
  36.0 9.3 %collective-permute-start.2 = (bf16[20,8,128]{2,1,0:T(8,128)(2,1)S(1)}, bf16[20,8,128]{2,1,0:T(8,128)(2,1)S(1)}, u32[]{:S(2)}, u32[]{:S(2)}) collective-permute-start(bf16[20,8,128]{2,1,0:T(8,128)(2,1)S(1)} %get-tuple-element.32), channel_id=1, source_target_pairs={{16,32},{48,64},{80,96},{112,128},{144,160},{176,192},{208,224},{2... | collective-permute-start | bytes 122888 | tf_op jit(solution)/shard_map/ppermute | solution.py:463
  45.3 3.5 %all-gather.2 = bf16[40,8,128]{2,1,0:T(8,128)(2,1)S(1)} all-gather(bf16[20,8,128]{2,1,0:T(8,128)(2,1)S(1)} %get-tuple-element.33), channel_id=4, replica_groups={{0,16},{32,48},{64,80},{96,112},{128,144},{160,176},{192,208},{224,240}..., dimensions={0}, use_global_device_ids=true | all-gather | bytes 122880 | tf_op jit(solution)/shard_map/all_gather | solution.py:464
  48.9 0.0 collective-permute-done.2.refs_6_.refs_8_
  48.9 0.1 shard_map.89
  49.0 9.6 %collective-permute-start.3 = (bf16[24,8,128]{2,1,0:T(8,128)(2,1)S(1)}, bf16[24,8,128]{2,1,0:T(8,128)(2,1)S(1)}, u32[]{:S(2)}, u32[]{:S(2)}) collective-permute-start(bf16[24,8,128]{2,1,0:T(8,128)(2,1)S(1)} %get-tuple-element.34), channel_id=1, source_target_pairs={{1,2},{3,4},{5,6},{7,8},{9,10},{11,12},{13,14},{2,1},{4,3},{6,5},{... | collective-permute-start | bytes 147464 | tf_op jit(solution)/shard_map/ppermute | solution.py:468
  58.6 0.1 add_convert_fusion.refs_0_
  58.7 1.9 %all-gather.3 = bf16[48,8,128]{2,1,0:T(8,128)(2,1)S(1)} all-gather(bf16[24,8,128]{2,1,0:T(8,128)(2,1)S(1)} %get-tuple-element.35), channel_id=5, replica_groups={{0,1},{2,3},{4,5},{6,7},{8,9},{10,11},{12,13},{14,15},{16,17},{18,19},{..., dimensions={0}, use_global_device_ids=true | all-gather | bytes 147456 | tf_op jit(solution)/shard_map/all_gather | solution.py:469
  60.6 0.2 collective-permute-done.3.refs_6_
  60.8 1.0 %shard_map.90 = (f32[320,128]{1,0:T(8,128)S(1)}, f32[128,128]{1,0:T(8,128)S(1)}, f32[32,128]{1,0:T(8,128)S(1)}, f32[128,128]{1,0:T(8,128)S(1)}) custom-call(f32[320,128]{1,0:T(8,128)S(1)} %get-tuple-element.31.refs_0_, f32[320,128]{1,0:T(8,128)S(1)} %get-tuple-element.22.refs_1_, bf16[5,5,8,8,128]{4,3,2,1,0:T(8,128)(2,1)S(1)} %get-tuple-element.23.refs_2_, ...), custom_call_target="tpu_custom_call" | custom-call | tf_op jit(solution)/shard_map/pallas_call | solution.py:421
  61.8 3.3 %all-gather.4 = f32[64,128]{1,0:T(8,128)S(1)} all-gather(f32[32,128]{1,0:T(8,128)S(1)} %get-tuple-element.38), channel_id=6, replica_groups={{0,16},{32,48},{64,80},{96,112},{128,144},{160,176},{192,208},{224,240}..., dimensions={0}, use_global_device_ids=true | all-gather | bytes 49152 | tf_op jit(solution)/shard_map/all_gather | solution.py:503
  65.1 0.8 shard_map.91
  65.9 18.4 %all-to-all-start = ((f32[32,4,128]{2,1,0:T(4,128)}), f32[32,4,128]{2,1,0:T(4,128)S(1)}, u32[]{:S(2)}, u32[]{:S(2)}) async-start(f32[32,4,128]{2,1,0:T(4,128)} %bitcast.10), calls=%async_computation | async-start | bytes 131072 | tf_op jit(solution)/shard_map/all_to_all | solution.py:520
  84.4 0.7 copy.23
  85.0 6.0 %all-to-all-done = f32[32,4,128]{2,1,0:T(4,128)S(1)} async-done(((f32[32,4,128]{2,1,0:T(4,128)}), f32[32,4,128]{2,1,0:T(4,128)S(1)}, u32[]{:S(2)}, u32[]{:S(2)}) %all-to-all-start) | async-done | bytes 65568 | tf_op jit(solution)/shard_map/all_to_all | solution.py:520
  91.1 0.1 copy.20
  91.2 0.1 copy.19
  91.4 0.1 select_add_fusion
  91.5 0.1 fusion.1
  91.6 0.1 slice_add_fusion.1
  91.8 0.5 copy.22
  92.3 0.9 broadcast_in_dim_reshape.3
  (9 shorter events, 0.1 us)
Async XLA Ops:
  2.3 12.4 %copy-start = (s32[16]{0:T(128)S(1)}, s32[16]{0:T(128)}, u32[]{:S(2)}) copy-start(s32[16]{0:T(128)} %param.13) | copy-start | bytes 196
  2.3 17.5 %collective-permute-start = (bf16[49,8,128]{2,1,0:T(8,128)(2,1)S(1)}, bf16[49,8,128]{2,1,0:T(8,128)(2,1)S(1)}, u32[]{:S(2)}, u32[]{:S(2)}) collective-permute-start(bf16[49,8,128]{2,1,0:T(8,128)(2,1)S(1)} %get-tuple-element.27), channel_id=1, source_target_pairs={{16,32},{48,64},{80,96},{112,128},{144,160},{176,192},{208,224},{2... | collective-permute-start | bytes 301064 | tf_op jit(solution)/shard_map/ppermute | solution.py:463
  19.9 15.1 %collective-permute-start.1 = (bf16[53,8,128]{2,1,0:T(8,128)(2,1)S(1)}, bf16[53,8,128]{2,1,0:T(8,128)(2,1)S(1)}, u32[]{:S(2)}, u32[]{:S(2)}) collective-permute-start(bf16[53,8,128]{2,1,0:T(8,128)(2,1)S(1)} %get-tuple-element.29), channel_id=1, source_target_pairs={{1,2},{3,4},{5,6},{7,8},{9,10},{11,12},{13,14},{2,1},{4,3},{6,5},{... | collective-permute-start | bytes 325640 | tf_op jit(solution)/shard_map/ppermute | solution.py:468
  36.0 12.8 %collective-permute-start.2 = (bf16[20,8,128]{2,1,0:T(8,128)(2,1)S(1)}, bf16[20,8,128]{2,1,0:T(8,128)(2,1)S(1)}, u32[]{:S(2)}, u32[]{:S(2)}) collective-permute-start(bf16[20,8,128]{2,1,0:T(8,128)(2,1)S(1)} %get-tuple-element.32), channel_id=1, source_target_pairs={{16,32},{48,64},{80,96},{112,128},{144,160},{176,192},{208,224},{2... | collective-permute-start | bytes 122888 | tf_op jit(solution)/shard_map/ppermute | solution.py:463
  49.0 11.8 %collective-permute-start.3 = (bf16[24,8,128]{2,1,0:T(8,128)(2,1)S(1)}, bf16[24,8,128]{2,1,0:T(8,128)(2,1)S(1)}, u32[]{:S(2)}, u32[]{:S(2)}) collective-permute-start(bf16[24,8,128]{2,1,0:T(8,128)(2,1)S(1)} %get-tuple-element.34), channel_id=1, source_target_pairs={{1,2},{3,4},{5,6},{7,8},{9,10},{11,12},{13,14},{2,1},{4,3},{6,5},{... | collective-permute-start | bytes 147464 | tf_op jit(solution)/shard_map/ppermute | solution.py:468
  65.9 25.2 %all-to-all-start = ((f32[32,4,128]{2,1,0:T(4,128)}), f32[32,4,128]{2,1,0:T(4,128)S(1)}, u32[]{:S(2)}, u32[]{:S(2)}) async-start(f32[32,4,128]{2,1,0:T(4,128)} %bitcast.10), calls=%async_computation | async-start | bytes 131072 | tf_op jit(solution)/shard_map/all_to_all | solution.py:520

commit v5 on v4

--- a/solution.py
+++ b/solution.py
@@ -358,10 +358,10 @@
         b = normal["B"] * y_edge(out, field, y_at_b)
         for ref, beyond in ((below, jnp.where(is_odd_b, a, b)), (above, jnp.where(is_odd_b, b, a))):
             even = 0.5 * beyond + 0.25 * shifted(beyond, 0)
-            ref[pl.ds(field * OUTER, 1), :] = jnp.zeros((1, LANES), f32)
+            ref[pl.ds(field, 1), :] = jnp.zeros((1, LANES), f32)
             for k in range(HALF):
-                ref[pl.ds(field * OUTER + 1 + k, 1), :] = even[2 * k : 2 * k + 1]
-            ref[pl.ds(field * OUTER + OUTER - 1, 1), :] = 0.25 * beyond[SIDE - 1 :]
+                ref[pl.ds((1 + k) * FIELDS + field, 1), :] = even[2 * k : 2 * k + 1]
+            ref[pl.ds((OUTER - 1) * FIELDS + field, 1), :] = 0.25 * beyond[SIDE - 1 :]
     for field in range(FIELDS):
         first, final = tile(out, field, 0), tile(out, field, SIDE - 1)
         f = normal["F"] * jnp.where(is_odd_l, final, first)
@@ -375,7 +375,7 @@
         coarse.append(0.5 * after + 0.25 * fine[SIDE - 1])
         for k in range(OUTER):
             value = coarse[k]
-            index = field * OUTER + k
+            index = k * FIELDS + field
             under = below[pl.ds(index, 1), :]
             even = 0.5 * value + 0.25 * shifted(value, 0)
             even = even + jnp.where(row == 0, jnp.broadcast_to(0.25 * under, (SIDE, LANES)), 0.0)
@@ -386,18 +386,20 @@
     count = FIELDS * OUTER
     own[pl.ds(0, count * HALF), :] = grid[pl.ds(0, count * HALF, stride=2), :]
     own[pl.ds(count * HALF, LANES - count * HALF), :] = jnp.zeros((LANES - count * HALF, LANES), f32)
-    b_row[pl.ds(count, LANES - count), :] = jnp.zeros((LANES - count, LANES), f32)
+    b_row[pl.ds(count, 2), :] = jnp.zeros((2, LANES), f32)
     a_row[pl.ds(count, 2), :] = jnp.zeros((2, LANES), f32)
 
 
-def send_kernel(odd, weights, own, a_got, b_row, send, rows):
+def send_kernel(odd, weights, own, a_got, b_row, send, rows, edge):
     odd_b = odd[1]
     count = FIELDS * OUTER
     rows[...] = own[...]
     at = pl.ds((1 - odd_b) * (HALF - 1), count, stride=HALF)
     rows[at, :] = rows[at, :] + a_got[1 - odd_b, pl.ds(0, count), :]
 
-    values = jnp.concatenate([rows[...], b_row[...]], 0)
+    edge[...] = jnp.zeros_like(edge)
+    edge[pl.ds((1 - odd_b) * (HALF - 1), count, stride=HALF), :] = b_row[pl.ds(0, count), :]
+    values = jnp.concatenate([rows[...], edge[...]], 0)
     size = weights.shape[0]
     total = jnp.zeros((size, 2 * LANES), f32)
     for _ in range(3):
@@ -410,6 +412,28 @@
     send[pl.ds(pl.multiple_of(odd_b * size, size), size), :] = total[:, LANES:]
 
 
+def final_kernel(bricks, odd, got, out, turned):
+    odd_b = odd[1]
+    brick = lax.axis_index("brick")
+    size = got.shape[0] // 2
+    own = got[pl.ds(pl.multiple_of((1 - odd_b) * size, size), size), :]
+    edge = got[pl.ds(pl.multiple_of(odd_b * size, size), size), :]
+    valid = (brick > 0) & (brick < bricks - 1)
+    total = own + jnp.where(valid, edge, 0.0)
+    turned[...] = jnp.concatenate([total, jnp.zeros((LANES - size, LANES), f32)], 0).T
+    cells = FIELDS * HALF
+    rows = 24
+    lane = lax.broadcasted_iota(jnp.int32, (rows, LANES), 1) % HALF
+    blocks = [turned[pl.ds(cells * x, rows), :] for x in range(OUTER)]
+    for k in range(HALF):
+        total = jnp.zeros((rows, LANES), f32)
+        for index, block in enumerate(blocks):
+            x = index - 1
+            moved = block if x == k else pltpu.roll(block, (x - k) % LANES, 1)
+            total = total + jnp.where(lane == x % HALF, moved, 0.0)
+        out[pl.ds(k, cells, stride=HALF), :] = total[:cells, : out.shape[1]]
+
+
 def call(kernel, outs, scratch, *args, resident=True):
     space = pltpu.VMEM if resident else pltpu.HBM
     args = [pltpu.with_memory_space_constraint(arg, space) for arg in args]
@@ -431,11 +455,6 @@
 def shards(adjoint, source, block, precond, couple, solid, coarse_owner):
     levels = lax.axis_size("level")
     bricks = lax.axis_size("brick")
-    brick = lax.axis_index("brick")
-    odd_b = brick % 2 == 1
-    fields = adjoint.shape[0]
-
-    b_valid = jnp.where(odd_b, brick < bricks - 1, brick > 0)
     b_route = both_ways(far_pairs(bricks))
     f_route = both_ways(far_pairs(levels))
     a_groups = near_pairs(bricks)
@@ -493,15 +512,15 @@
     )
     f_got, n_got = level_exchange(f_send, n_send)
     square = ((LANES, LANES), f32)
+    edge_rows = ((FIELDS * OUTER + 2, LANES), f32)
     smoothed, own, a_row, b_row = call(
-        last_kernel, [whole, square, ((FIELDS * OUTER + 2, LANES), f32), square],
+        last_kernel, [whole, square, edge_rows, edge_rows],
         [whole[0], strip, strip, strip, strip, corner, (FIELDS * OUTER * SIDE, LANES),
          (FIELDS * OUTER + 2, LANES), (FIELDS * OUTER + 2, LANES)],
         cells, *params, f_got, n_got, b_got, a_got, *old,
     )
     smoothed = smoothed.reshape(adjoint.shape)
     a_got = lax.all_gather(a_row, "brick", axis_index_groups=a_groups)
-    half_x, half_y = HALF, HALF
 
     nz = adjoint.shape[3]
     zblock = nz // (2 * levels)
@@ -514,32 +533,18 @@
     )
 
     (send,) = call(
-        send_kernel, [square], [square[0]], weights.astype(bf16), own, a_got, b_row
+        send_kernel, [square], [square[0], square[0]], weights.astype(bf16), own, a_got, b_row
     )
     send = send.reshape(2 * levels, zblock, LANES)
     got = lax.all_to_all(
         send, BOTH, split_axis=0, concat_axis=0, tiled=True, axis_index_groups=columns
     )
-    own_got = jnp.where(odd_b, got[:levels], got[levels:])
-    edge_got = jnp.where(odd_b, got[levels:], got[:levels])
-    rows = fields * (half_x + 2)
-    own_got = own_got[..., : rows * half_y].reshape(levels, zblock, fields, half_x + 2, half_y)
-    edge_got = edge_got[..., :rows].reshape(levels, zblock, fields, half_x + 2, 1)
-    b_at = jnp.where(odd_b, half_y - 1, 0)
-    rest = jnp.where((jnp.arange(half_y) == b_at) & b_valid, edge_got, 0.0)
-    total = own_got + rest
-    up = total[:-1, :, :, -1:]
-    down = total[1:, :, :, :1]
-    none = jnp.zeros_like(total[:1, :, :, :1])
-    up = jnp.concatenate([none, up], 0)
-    down = jnp.concatenate([down, none], 0)
-    body = total[:, :, :, 1:-1]
-    body = jnp.concatenate(
-        [body[:, :, :, :1] + up, body[:, :, :, 1:-1], body[:, :, :, -1:] + down], 3
-    )
-    coarse_rhs = body.transpose(2, 0, 3, 4, 1).reshape(
-        fields, levels * half_x, half_y, zblock
-    )[None]
+    (coarse_rhs,) = call(
+        functools.partial(final_kernel, bricks), [((FIELDS * HALF * zblock, levels * HALF), f32)],
+        [square[0]], got.reshape(LANES, LANES),
+    )
+    coarse_rhs = coarse_rhs.reshape(FIELDS, HALF, zblock, levels * HALF)
+    coarse_rhs = coarse_rhs.transpose(0, 3, 1, 2)[None]
     return (smoothed, coarse_rhs)
 
 

time: 93.6 us -> 92.3 us (0.986)
  local copies, waits for them, and re-layouts: 2.57 us -> 1.38 us
    pallas_call x6 -> x7, Pallas kernels: 4.78 us -> 5.02 us  [call(): pl.pallas_call(body, out_shape=[pltpu.VMEM(shape, dtype) for shape, dtype...]
where the time goes in v5:
time: 92.3 us; the launch traced here: 91.9 us
  starting transfers between devices  62.1 us (67%)
  blocking collectives  15.6 us (17%)
  waiting for transfers between devices  6.82 us (7%)
  Pallas kernels  5.02 us (5%)
  local copies, waits for them, and re-layouts  1.38 us (1%)
    ppermute x2, starting transfers between devices, level_exchange(): f_got = lax.ppermute(f_send, 'level', f_route)  22.1 us
    ppermute x2, starting transfers between devices, brick_exchange(): b_got = lax.ppermute(b_send, 'brick', b_route)  21.6 us
    all_to_all x1, starting transfers between devices, shards(): lax.all_to_all(send, BOTH, split_axis=0, concat_axis=0, tiled=True, axis_...  18.4 us
    all_gather x2, blocking collectives, brick_exchange(): a_got = lax.all_gather(a_send, 'brick', axis_index_groups=a_groups)  8.52 us
    all_to_all x1, waiting for transfers between devices, shards(): lax.all_to_all(send, BOTH, split_axis=0, concat_axis=0, tiled=True, axis_...  6.08 us
    pallas_call x7, Pallas kernels, call(): pl.pallas_call(body, out_shape=[pltpu.VMEM(shape, dtype) for shape, dtype...  5.02 us
    all_gather x2, blocking collectives, level_exchange(): n_got = lax.all_gather(n_send, 'level', axis_index_groups=n_groups)  3.84 us
    all_gather x1, blocking collectives, shards(): a_got = lax.all_gather(a_row, 'brick', axis_index_groups=a_groups)  3.25 us
  transfers between devices with their start and end apart: 5, of which 3 were waited for; matrix products, arithmetic and copies ran while one was open for 1% of the time, Pallas kernels for 0%

profile of v5, /device:TPU:33, one launch (start us, length us, event | category | flops | bytes accessed | tf_op | source)
XLA Modules:
  0.0 91.9 jit_solution(4383456858813185616)
XLA Ops:
  0.6 1.6 %shard_map.86 = (f32[320,128]{1,0:T(8,128)S(1)}, f32[320,128]{1,0:T(8,128)S(1)}, bf16[5,5,8,8,128]{4,3,2,1,0:T(8,128)(2,1)S(1)}, bf16[5,5,8,8,128]{4,3,2,1,0:T(8...) custom-call(f32[320,128]{1,0:T(8,128)} %bitcast.29, ...), custom_call_target="tpu_custom_call" | custom-call | tf_op jit(solution)/shard_map/pallas_call | solution.py:445
  2.3 0.0 copy-start
  2.3 12.3 %collective-permute-start = (bf16[49,8,128]{2,1,0:T(8,128)(2,1)S(1)}, bf16[49,8,128]{2,1,0:T(8,128)(2,1)S(1)}, u32[]{:S(2)}, u32[]{:S(2)}) collective-permute-start(bf16[49,8,128]{2,1,0:T(8,128)(2,1)S(1)} %get-tuple-element.27), channel_id=1, source_target_pairs={{16,32},{48,64},{80,96},{112,128},{144,160},{176,192},{208,224},{2... | collective-permute-start | bytes 301064 | tf_op jit(solution)/shard_map/ppermute | solution.py:482
  14.6 0.0 copy-done
  14.6 0.1 select_reduce_fusion
  14.8 5.0 %all-gather = bf16[98,8,128]{2,1,0:T(8,128)(2,1)S(1)} all-gather(bf16[49,8,128]{2,1,0:T(8,128)(2,1)S(1)} %get-tuple-element.28), channel_id=2, replica_groups={{0,16},{32,48},{64,80},{96,112},{128,144},{160,176},{192,208},{224,240}..., dimensions={0}, use_global_device_ids=true | all-gather | bytes 301056 | tf_op jit(solution)/shard_map/all_gather | solution.py:483
  19.8 0.0 collective-permute-done.refs_6_.refs_8_.refs_12_
  19.8 0.1 shard_map.87
  19.9 12.4 %collective-permute-start.1 = (bf16[53,8,128]{2,1,0:T(8,128)(2,1)S(1)}, bf16[53,8,128]{2,1,0:T(8,128)(2,1)S(1)}, u32[]{:S(2)}, u32[]{:S(2)}) collective-permute-start(bf16[53,8,128]{2,1,0:T(8,128)(2,1)S(1)} %get-tuple-element.29), channel_id=1, source_target_pairs={{1,2},{3,4},{5,6},{7,8},{9,10},{11,12},{13,14},{2,1},{4,3},{6,5},{... | collective-permute-start | bytes 325640 | tf_op jit(solution)/shard_map/ppermute | solution.py:487
  32.3 0.1 add_multiply_fusion
  32.4 0.1 mul.29
  32.5 2.0 %all-gather.1 = bf16[106,8,128]{2,1,0:T(8,128)(2,1)S(1)} all-gather(bf16[53,8,128]{2,1,0:T(8,128)(2,1)S(1)} %get-tuple-element.30), channel_id=3, replica_groups={{0,1},{2,3},{4,5},{6,7},{8,9},{10,11},{12,13},{14,15},{16,17},{18,19},{..., dimensions={0}, use_global_device_ids=true | all-gather | bytes 325632 | tf_op jit(solution)/shard_map/all_gather | solution.py:488
  34.5 0.6 collective-permute-done.1.refs_6_.refs_10_
  35.0 1.0 %shard_map.88 = (f32[320,128]{1,0:T(8,128)S(1)}, bf16[20,8,128]{2,1,0:T(8,128)(2,1)S(1)}, bf16[20,8,128]{2,1,0:T(8,128)(2,1)S(1)}) custom-call(f32[320,128]{1,0:T(8,128)S(1)} %get-tuple-element.21.refs_0_, f32[320,128]{1,0:T(8,128)S(1)} %get-tuple-element.22.refs_1_, bf16[5,5,8,8,128]{4,3,2,1,0:T(8,128)(2,1)S(1)} %get-tuple-element.23.refs_2_, ...), custom_call_target="tpu_custom_call" | custom-call | tf_op jit(solution)/shard_map/pallas_call | solution.py:445
  36.0 9.3 %collective-permute-start.2 = (bf16[20,8,128]{2,1,0:T(8,128)(2,1)S(1)}, bf16[20,8,128]{2,1,0:T(8,128)(2,1)S(1)}, u32[]{:S(2)}, u32[]{:S(2)}) collective-permute-start(bf16[20,8,128]{2,1,0:T(8,128)(2,1)S(1)} %get-tuple-element.32), channel_id=1, source_target_pairs={{16,32},{48,64},{80,96},{112,128},{144,160},{176,192},{208,224},{2... | collective-permute-start | bytes 122888 | tf_op jit(solution)/shard_map/ppermute | solution.py:482
  45.3 3.5 %all-gather.2 = bf16[40,8,128]{2,1,0:T(8,128)(2,1)S(1)} all-gather(bf16[20,8,128]{2,1,0:T(8,128)(2,1)S(1)} %get-tuple-element.33), channel_id=4, replica_groups={{0,16},{32,48},{64,80},{96,112},{128,144},{160,176},{192,208},{224,240}..., dimensions={0}, use_global_device_ids=true | all-gather | bytes 122880 | tf_op jit(solution)/shard_map/all_gather | solution.py:483
  48.9 0.0 collective-permute-done.2.refs_6_.refs_8_
  48.9 0.1 shard_map.89
  49.0 9.6 %collective-permute-start.3 = (bf16[24,8,128]{2,1,0:T(8,128)(2,1)S(1)}, bf16[24,8,128]{2,1,0:T(8,128)(2,1)S(1)}, u32[]{:S(2)}, u32[]{:S(2)}) collective-permute-start(bf16[24,8,128]{2,1,0:T(8,128)(2,1)S(1)} %get-tuple-element.34), channel_id=1, source_target_pairs={{1,2},{3,4},{5,6},{7,8},{9,10},{11,12},{13,14},{2,1},{4,3},{6,5},{... | collective-permute-start | bytes 147464 | tf_op jit(solution)/shard_map/ppermute | solution.py:487
  58.6 0.1 add_convert_fusion.refs_0_
  58.7 1.9 %all-gather.3 = bf16[48,8,128]{2,1,0:T(8,128)(2,1)S(1)} all-gather(bf16[24,8,128]{2,1,0:T(8,128)(2,1)S(1)} %get-tuple-element.35), channel_id=5, replica_groups={{0,1},{2,3},{4,5},{6,7},{8,9},{10,11},{12,13},{14,15},{16,17},{18,19},{..., dimensions={0}, use_global_device_ids=true | all-gather | bytes 147456 | tf_op jit(solution)/shard_map/all_gather | solution.py:488
  60.6 0.2 collective-permute-done.3.refs_6_
  60.8 1.0 %shard_map.90 = (f32[320,128]{1,0:T(8,128)S(1)}, f32[128,128]{1,0:T(8,128)S(1)}, f32[32,128]{1,0:T(8,128)S(1)}, f32[32,128]{1,0:T(8,128)S(1)}) custom-call(f32[320,128]{1,0:T(8,128)S(1)} %get-tuple-element.31.refs_0_, f32[320,128]{1,0:T(8,128)S(1)} %get-tuple-element.22.refs_1_, bf16[5,5,8,8,128]{4,3,2,1,0:T(8,128)(2,1)S(1)} %get-tuple-element.23.refs_2_, ...), custom_call_target="tpu_custom_call" | custom-call | tf_op jit(solution)/shard_map/pallas_call | solution.py:445
  61.8 3.2 %all-gather.4 = f32[64,128]{1,0:T(8,128)S(1)} all-gather(f32[32,128]{1,0:T(8,128)S(1)} %get-tuple-element.38), channel_id=6, replica_groups={{0,16},{32,48},{64,80},{96,112},{128,144},{160,176},{192,208},{224,240}..., dimensions={0}, use_global_device_ids=true | all-gather | bytes 49152 | tf_op jit(solution)/shard_map/all_gather | solution.py:523
  65.0 0.9 shard_map.91
  65.9 18.4 %all-to-all-start = ((f32[32,4,128]{2,1,0:T(4,128)}), f32[32,4,128]{2,1,0:T(4,128)S(1)}, u32[]{:S(2)}, u32[]{:S(2)}) async-start(f32[32,4,128]{2,1,0:T(4,128)} %bitcast.10), calls=%async_computation | async-start | bytes 131072 | tf_op jit(solution)/shard_map/all_to_all | solution.py:539
  84.3 0.7 copy.9
  85.0 6.1 %all-to-all-done = f32[32,4,128]{2,1,0:T(4,128)S(1)} async-done(((f32[32,4,128]{2,1,0:T(4,128)}), f32[32,4,128]{2,1,0:T(4,128)S(1)}, u32[]{:S(2)}, u32[]{:S(2)}) %all-to-all-start) | async-done | bytes 65568 | tf_op jit(solution)/shard_map/all_to_all | solution.py:539
  91.1 0.2 shard_map.92
  91.3 0.6 copy.10
  (2 shorter events, 0.0 us)
Async XLA Ops:
  2.3 12.4 %copy-start = (s32[16]{0:T(128)S(1)}, s32[16]{0:T(128)}, u32[]{:S(2)}) copy-start(s32[16]{0:T(128)} %param.13) | copy-start | bytes 196
  2.3 17.5 %collective-permute-start = (bf16[49,8,128]{2,1,0:T(8,128)(2,1)S(1)}, bf16[49,8,128]{2,1,0:T(8,128)(2,1)S(1)}, u32[]{:S(2)}, u32[]{:S(2)}) collective-permute-start(bf16[49,8,128]{2,1,0:T(8,128)(2,1)S(1)} %get-tuple-element.27), channel_id=1, source_target_pairs={{16,32},{48,64},{80,96},{112,128},{144,160},{176,192},{208,224},{2... | collective-permute-start | bytes 301064 | tf_op jit(solution)/shard_map/ppermute | solution.py:482
  19.9 15.1 %collective-permute-start.1 = (bf16[53,8,128]{2,1,0:T(8,128)(2,1)S(1)}, bf16[53,8,128]{2,1,0:T(8,128)(2,1)S(1)}, u32[]{:S(2)}, u32[]{:S(2)}) collective-permute-start(bf16[53,8,128]{2,1,0:T(8,128)(2,1)S(1)} %get-tuple-element.29), channel_id=1, source_target_pairs={{1,2},{3,4},{5,6},{7,8},{9,10},{11,12},{13,14},{2,1},{4,3},{6,5},{... | collective-permute-start | bytes 325640 | tf_op jit(solution)/shard_map/ppermute | solution.py:487
  36.0 12.8 %collective-permute-start.2 = (bf16[20,8,128]{2,1,0:T(8,128)(2,1)S(1)}, bf16[20,8,128]{2,1,0:T(8,128)(2,1)S(1)}, u32[]{:S(2)}, u32[]{:S(2)}) collective-permute-start(bf16[20,8,128]{2,1,0:T(8,128)(2,1)S(1)} %get-tuple-element.32), channel_id=1, source_target_pairs={{16,32},{48,64},{80,96},{112,128},{144,160},{176,192},{208,224},{2... | collective-permute-start | bytes 122888 | tf_op jit(solution)/shard_map/ppermute | solution.py:482
  49.0 11.8 %collective-permute-start.3 = (bf16[24,8,128]{2,1,0:T(8,128)(2,1)S(1)}, bf16[24,8,128]{2,1,0:T(8,128)(2,1)S(1)}, u32[]{:S(2)}, u32[]{:S(2)}) collective-permute-start(bf16[24,8,128]{2,1,0:T(8,128)(2,1)S(1)} %get-tuple-element.34), channel_id=1, source_target_pairs={{1,2},{3,4},{5,6},{7,8},{9,10},{11,12},{13,14},{2,1},{4,3},{6,5},{... | collective-permute-start | bytes 147464 | tf_op jit(solution)/shard_map/ppermute | solution.py:487
  65.9 25.2 %all-to-all-start = ((f32[32,4,128]{2,1,0:T(4,128)}), f32[32,4,128]{2,1,0:T(4,128)S(1)}, u32[]{:S(2)}, u32[]{:S(2)}) async-start(f32[32,4,128]{2,1,0:T(4,128)} %bitcast.10), calls=%async_computation | async-start | bytes 131072 | tf_op jit(solution)/shard_map/all_to_all | solution.py:539

commit v6 on v5

--- a/solution.py
+++ b/solution.py
@@ -333,8 +333,8 @@
 
 def last_kernel(
     odd, s, source, block, precond, couple, solid, f_got, n_got, b_got, a_got, f_old, n_old, b_old, a_old,
-    out, own, a_row, b_row,
-    middle, low, high, x_low, x_high, corners, grid, below, above,
+    weights, out, own, to_a, to_b,
+    middle, low, high, x_low, x_high, corners, grid, below, above, a_row, b_row, stacked,
 ):
     ins = Cells(source, block, precond, couple, solid)
     got = readers(odd, f_got, n_got, b_got, a_got)
@@ -384,32 +384,28 @@
             a_row[pl.ds(index, 1), :] = jnp.where(is_odd_b, 0.25 * under, over)
             b_row[pl.ds(index, 1), :] = jnp.where(is_odd_b, over, 0.25 * under)
     count = FIELDS * OUTER
-    own[pl.ds(0, count * HALF), :] = grid[pl.ds(0, count * HALF, stride=2), :]
-    own[pl.ds(count * HALF, LANES - count * HALF), :] = jnp.zeros((LANES - count * HALF, LANES), f32)
-    b_row[pl.ds(count, 2), :] = jnp.zeros((2, LANES), f32)
-    a_row[pl.ds(count, 2), :] = jnp.zeros((2, LANES), f32)
-
-
-def send_kernel(odd, weights, own, a_got, b_row, send, rows, edge):
-    odd_b = odd[1]
-    count = FIELDS * OUTER
-    rows[...] = own[...]
-    at = pl.ds((1 - odd_b) * (HALF - 1), count, stride=HALF)
-    rows[at, :] = rows[at, :] + a_got[1 - odd_b, pl.ds(0, count), :]
-
-    edge[...] = jnp.zeros_like(edge)
-    edge[pl.ds((1 - odd_b) * (HALF - 1), count, stride=HALF), :] = b_row[pl.ds(0, count), :]
-    values = jnp.concatenate([rows[...], edge[...]], 0)
-    size = weights.shape[0]
-    total = jnp.zeros((size, 2 * LANES), f32)
+    stacked[...] = jnp.zeros_like(stacked)
+    stacked[pl.ds(0, count * HALF), :] = grid[pl.ds(0, count * HALF, stride=2), :]
+    for start, at, ref in ((LANES, odd_b, a_row), (2 * LANES, 1 - odd_b, b_row)):
+        stacked[pl.ds(start + at * (HALF - 1), count, stride=HALF), :] = ref[pl.ds(0, count), :]
+    values = stacked[...]
+    total = jnp.zeros((weights.shape[0], 3 * LANES), f32)
     for _ in range(3):
         part = values.astype(jnp.bfloat16)
         values = values - part.astype(f32)
         total = total + lax.dot_general(
             weights[...], part, (((1,), (1,)), ((), ())), preferred_element_type=f32
         )
-    send[pl.ds(pl.multiple_of((1 - odd_b) * size, size), size), :] = total[:, :LANES]
-    send[pl.ds(pl.multiple_of(odd_b * size, size), size), :] = total[:, LANES:]
+    own[...] = total[:, :LANES]
+    to_a[...] = total[:, LANES : 2 * LANES]
+    to_b[...] = total[:, 2 * LANES :]
+
+
+def send_kernel(odd, own, a_got, to_b, send):
+    odd_b = odd[1]
+    size = own.shape[0]
+    send[pl.ds(pl.multiple_of((1 - odd_b) * size, size), size), :] = own[...] + a_got[1 - odd_b]
+    send[pl.ds(pl.multiple_of(odd_b * size, size), size), :] = to_b[...]
 
 
 def final_kernel(bricks, odd, got, out, turned):
@@ -511,17 +507,6 @@
         [strip, strip, (SIDE, LANES)], cells, *params, b_got, a_got,
     )
     f_got, n_got = level_exchange(f_send, n_send)
-    square = ((LANES, LANES), f32)
-    edge_rows = ((FIELDS * OUTER + 2, LANES), f32)
-    smoothed, own, a_row, b_row = call(
-        last_kernel, [whole, square, edge_rows, edge_rows],
-        [whole[0], strip, strip, strip, strip, corner, (FIELDS * OUTER * SIDE, LANES),
-         (FIELDS * OUTER + 2, LANES), (FIELDS * OUTER + 2, LANES)],
-        cells, *params, f_got, n_got, b_got, a_got, *old,
-    )
-    smoothed = smoothed.reshape(adjoint.shape)
-    a_got = lax.all_gather(a_row, "brick", axis_index_groups=a_groups)
-
     nz = adjoint.shape[3]
     zblock = nz // (2 * levels)
     slots = jnp.arange(levels, dtype=jnp.int32)
@@ -532,9 +517,18 @@
         (fine == 2 * target + 1) | (fine == 2 * target - 1), 0.25, 0.0
     )
 
-    (send,) = call(
-        send_kernel, [square], [square[0], square[0]], weights.astype(bf16), own, a_got, b_row
-    )
+    square = ((LANES, LANES), f32)
+    half = ((levels * zblock, LANES), f32)
+    edge_rows = (FIELDS * OUTER + 2, LANES)
+    smoothed, own, to_a, to_b = call(
+        last_kernel, [whole, half, half, half],
+        [whole[0], strip, strip, strip, strip, corner, (FIELDS * OUTER * SIDE, LANES),
+         edge_rows, edge_rows, edge_rows, edge_rows, (3 * LANES, LANES)],
+        cells, *params, f_got, n_got, b_got, a_got, *old, weights.astype(bf16),
+    )
+    smoothed = smoothed.reshape(adjoint.shape)
+    a_got = lax.all_gather(to_a, "brick", axis_index_groups=a_groups)
+    (send,) = call(send_kernel, [square], [], own, a_got, to_b)
     send = send.reshape(2 * levels, zblock, LANES)
     got = lax.all_to_all(
         send, BOTH, split_axis=0, concat_axis=0, tiled=True, axis_index_groups=columns

time: 92.3 us -> 92.5 us (level)
  no operation moved by 1% of the time
where the time goes in v6:
time: 92.5 us; the launch traced here: 92.2 us
  starting transfers between devices  62.1 us (67%)
  blocking collectives  15.8 us (17%)
  waiting for transfers between devices  6.82 us (7%)
  Pallas kernels  5.06 us (5%)
  local copies, waits for them, and re-layouts  1.38 us (1%)
    ppermute x2, starting transfers between devices, level_exchange(): f_got = lax.ppermute(f_send, 'level', f_route)  22.1 us
    ppermute x2, starting transfers between devices, brick_exchange(): b_got = lax.ppermute(b_send, 'brick', b_route)  21.6 us
    all_to_all x1, starting transfers between devices, shards(): lax.all_to_all(send, BOTH, split_axis=0, concat_axis=0, tiled=True, axis_...  18.4 us
    all_gather x2, blocking collectives, brick_exchange(): a_got = lax.all_gather(a_send, 'brick', axis_index_groups=a_groups)  8.52 us
    all_to_all x1, waiting for transfers between devices, shards(): lax.all_to_all(send, BOTH, split_axis=0, concat_axis=0, tiled=True, axis_...  6.08 us
    pallas_call x7, Pallas kernels, call(): pl.pallas_call(body, out_shape=[pltpu.VMEM(shape, dtype) for shape, dtype...  5.06 us
    all_gather x2, blocking collectives, level_exchange(): n_got = lax.all_gather(n_send, 'level', axis_index_groups=n_groups)  3.84 us
    all_gather x1, blocking collectives, shards(): a_got = lax.all_gather(to_a, 'brick', axis_index_groups=a_groups)  3.43 us
  transfers between devices with their start and end apart: 5, of which 3 were waited for; matrix products, arithmetic and copies ran while one was open for 1% of the time, Pallas kernels for 0%

profile of v6, /device:TPU:33, one launch (start us, length us, event | category | flops | bytes accessed | tf_op | source)
XLA Modules:
  0.0 92.2 jit_solution(249848852410879309)
XLA Ops:
  0.6 1.6 %shard_map.86 = (f32[320,128]{1,0:T(8,128)S(1)}, f32[320,128]{1,0:T(8,128)S(1)}, bf16[5,5,8,8,128]{4,3,2,1,0:T(8,128)(2,1)S(1)}, bf16[5,5,8,8,128]{4,3,2,1,0:T(8...) custom-call(f32[320,128]{1,0:T(8,128)} %bitcast.29, ...), custom_call_target="tpu_custom_call" | custom-call | tf_op jit(solution)/shard_map/pallas_call | solution.py:441
  2.3 0.0 copy-start
  2.3 12.3 %collective-permute-start = (bf16[49,8,128]{2,1,0:T(8,128)(2,1)S(1)}, bf16[49,8,128]{2,1,0:T(8,128)(2,1)S(1)}, u32[]{:S(2)}, u32[]{:S(2)}) collective-permute-start(bf16[49,8,128]{2,1,0:T(8,128)(2,1)S(1)} %get-tuple-element.27), channel_id=1, source_target_pairs={{16,32},{48,64},{80,96},{112,128},{144,160},{176,192},{208,224},{2... | collective-permute-start | bytes 301064 | tf_op jit(solution)/shard_map/ppermute | solution.py:478
  14.6 0.0 copy-done
  14.6 0.1 select_reduce_fusion
  14.8 5.0 %all-gather = bf16[98,8,128]{2,1,0:T(8,128)(2,1)S(1)} all-gather(bf16[49,8,128]{2,1,0:T(8,128)(2,1)S(1)} %get-tuple-element.28), channel_id=2, replica_groups={{0,16},{32,48},{64,80},{96,112},{128,144},{160,176},{192,208},{224,240}..., dimensions={0}, use_global_device_ids=true | all-gather | bytes 301056 | tf_op jit(solution)/shard_map/all_gather | solution.py:479
  19.8 0.0 collective-permute-done.refs_6_.refs_8_.refs_12_
  19.8 0.1 shard_map.87
  19.9 12.4 %collective-permute-start.1 = (bf16[53,8,128]{2,1,0:T(8,128)(2,1)S(1)}, bf16[53,8,128]{2,1,0:T(8,128)(2,1)S(1)}, u32[]{:S(2)}, u32[]{:S(2)}) collective-permute-start(bf16[53,8,128]{2,1,0:T(8,128)(2,1)S(1)} %get-tuple-element.29), channel_id=1, source_target_pairs={{1,2},{3,4},{5,6},{7,8},{9,10},{11,12},{13,14},{2,1},{4,3},{6,5},{... | collective-permute-start | bytes 325640 | tf_op jit(solution)/shard_map/ppermute | solution.py:483
  32.3 0.1 add_multiply_fusion
  32.4 0.1 mul.29
  32.5 2.0 %all-gather.1 = bf16[106,8,128]{2,1,0:T(8,128)(2,1)S(1)} all-gather(bf16[53,8,128]{2,1,0:T(8,128)(2,1)S(1)} %get-tuple-element.30), channel_id=3, replica_groups={{0,1},{2,3},{4,5},{6,7},{8,9},{10,11},{12,13},{14,15},{16,17},{18,19},{..., dimensions={0}, use_global_device_ids=true | all-gather | bytes 325632 | tf_op jit(solution)/shard_map/all_gather | solution.py:484
  34.5 0.6 collective-permute-done.1.refs_6_.refs_10_
  35.0 1.0 %shard_map.88 = (f32[320,128]{1,0:T(8,128)S(1)}, bf16[20,8,128]{2,1,0:T(8,128)(2,1)S(1)}, bf16[20,8,128]{2,1,0:T(8,128)(2,1)S(1)}) custom-call(f32[320,128]{1,0:T(8,128)S(1)} %get-tuple-element.21.refs_0_, f32[320,128]{1,0:T(8,128)S(1)} %get-tuple-element.22.refs_1_, bf16[5,5,8,8,128]{4,3,2,1,0:T(8,128)(2,1)S(1)} %get-tuple-element.23.refs_2_, ...), custom_call_target="tpu_custom_call" | custom-call | tf_op jit(solution)/shard_map/pallas_call | solution.py:441
  36.0 9.3 %collective-permute-start.2 = (bf16[20,8,128]{2,1,0:T(8,128)(2,1)S(1)}, bf16[20,8,128]{2,1,0:T(8,128)(2,1)S(1)}, u32[]{:S(2)}, u32[]{:S(2)}) collective-permute-start(bf16[20,8,128]{2,1,0:T(8,128)(2,1)S(1)} %get-tuple-element.32), channel_id=1, source_target_pairs={{16,32},{48,64},{80,96},{112,128},{144,160},{176,192},{208,224},{2... | collective-permute-start | bytes 122888 | tf_op jit(solution)/shard_map/ppermute | solution.py:478
  45.3 3.5 %all-gather.2 = bf16[40,8,128]{2,1,0:T(8,128)(2,1)S(1)} all-gather(bf16[20,8,128]{2,1,0:T(8,128)(2,1)S(1)} %get-tuple-element.33), channel_id=4, replica_groups={{0,16},{32,48},{64,80},{96,112},{128,144},{160,176},{192,208},{224,240}..., dimensions={0}, use_global_device_ids=true | all-gather | bytes 122880 | tf_op jit(solution)/shard_map/all_gather | solution.py:479
  48.9 0.0 collective-permute-done.2.refs_6_.refs_8_
  48.9 0.1 shard_map.89
  49.0 9.6 %collective-permute-start.3 = (bf16[24,8,128]{2,1,0:T(8,128)(2,1)S(1)}, bf16[24,8,128]{2,1,0:T(8,128)(2,1)S(1)}, u32[]{:S(2)}, u32[]{:S(2)}) collective-permute-start(bf16[24,8,128]{2,1,0:T(8,128)(2,1)S(1)} %get-tuple-element.34), channel_id=1, source_target_pairs={{1,2},{3,4},{5,6},{7,8},{9,10},{11,12},{13,14},{2,1},{4,3},{6,5},{... | collective-permute-start | bytes 147464 | tf_op jit(solution)/shard_map/ppermute | solution.py:483
  58.6 0.1 add_convert_fusion.refs_14_
  58.7 1.9 %all-gather.3 = bf16[48,8,128]{2,1,0:T(8,128)(2,1)S(1)} all-gather(bf16[24,8,128]{2,1,0:T(8,128)(2,1)S(1)} %get-tuple-element.35), channel_id=5, replica_groups={{0,1},{2,3},{4,5},{6,7},{8,9},{10,11},{12,13},{14,15},{16,17},{18,19},{..., dimensions={0}, use_global_device_ids=true | all-gather | bytes 147456 | tf_op jit(solution)/shard_map/all_gather | solution.py:484
  60.6 0.2 collective-permute-done.3.refs_6_
  60.8 1.3 %shard_map.90 = (f32[320,128]{1,0:T(8,128)S(1)}, f32[64,128]{1,0:T(8,128)S(1)}, f32[64,128]{1,0:T(8,128)S(1)}, f32[64,128]{1,0:T(8,128)S(1)}) custom-call(f32[320,128]{1,0:T(8,128)S(1)} %get-tuple-element.31.refs_0_, f32[320,128]{1,0:T(8,128)S(1)} %get-tuple-element.22.refs_1_, bf16[5,5,8,8,128]{4,3,2,1,0:T(8,128)(2,1)S(1)} %get-tuple-element.23.refs_2_, ...), custom_call_target="tpu_custom_call" | custom-call | tf_op jit(solution)/shard_map/pallas_call | solution.py:441
  62.1 3.4 %all-gather.4 = f32[128,128]{1,0:T(8,128)S(1)} all-gather(f32[64,128]{1,0:T(8,128)S(1)} %get-tuple-element.38), channel_id=6, replica_groups={{0,16},{32,48},{64,80},{96,112},{128,144},{160,176},{192,208},{224,240}..., dimensions={0}, use_global_device_ids=true | all-gather | bytes 98304 | tf_op jit(solution)/shard_map/all_gather | solution.py:530
  65.5 0.6 shard_map.91
  66.1 18.4 %all-to-all-start = ((f32[32,4,128]{2,1,0:T(4,128)}), f32[32,4,128]{2,1,0:T(4,128)S(1)}, u32[]{:S(2)}, u32[]{:S(2)}) async-start(f32[32,4,128]{2,1,0:T(4,128)} %bitcast.10), calls=%async_computation | async-start | bytes 131072 | tf_op jit(solution)/shard_map/all_to_all | solution.py:533
  84.6 0.7 copy.9
  85.2 6.1 %all-to-all-done = f32[32,4,128]{2,1,0:T(4,128)S(1)} async-done(((f32[32,4,128]{2,1,0:T(4,128)}), f32[32,4,128]{2,1,0:T(4,128)S(1)}, u32[]{:S(2)}, u32[]{:S(2)}) %all-to-all-start) | async-done | bytes 65568 | tf_op jit(solution)/shard_map/all_to_all | solution.py:533
  91.3 0.2 shard_map.92
  91.6 0.6 copy.10
  (2 shorter events, 0.0 us)
Async XLA Ops:
  2.3 12.4 %copy-start = (s32[16]{0:T(128)S(1)}, s32[16]{0:T(128)}, u32[]{:S(2)}) copy-start(s32[16]{0:T(128)} %param.13) | copy-start | bytes 196
  2.3 17.5 %collective-permute-start = (bf16[49,8,128]{2,1,0:T(8,128)(2,1)S(1)}, bf16[49,8,128]{2,1,0:T(8,128)(2,1)S(1)}, u32[]{:S(2)}, u32[]{:S(2)}) collective-permute-start(bf16[49,8,128]{2,1,0:T(8,128)(2,1)S(1)} %get-tuple-element.27), channel_id=1, source_target_pairs={{16,32},{48,64},{80,96},{112,128},{144,160},{176,192},{208,224},{2... | collective-permute-start | bytes 301064 | tf_op jit(solution)/shard_map/ppermute | solution.py:478
  19.9 15.1 %collective-permute-start.1 = (bf16[53,8,128]{2,1,0:T(8,128)(2,1)S(1)}, bf16[53,8,128]{2,1,0:T(8,128)(2,1)S(1)}, u32[]{:S(2)}, u32[]{:S(2)}) collective-permute-start(bf16[53,8,128]{2,1,0:T(8,128)(2,1)S(1)} %get-tuple-element.29), channel_id=1, source_target_pairs={{1,2},{3,4},{5,6},{7,8},{9,10},{11,12},{13,14},{2,1},{4,3},{6,5},{... | collective-permute-start | bytes 325640 | tf_op jit(solution)/shard_map/ppermute | solution.py:483
  36.0 12.8 %collective-permute-start.2 = (bf16[20,8,128]{2,1,0:T(8,128)(2,1)S(1)}, bf16[20,8,128]{2,1,0:T(8,128)(2,1)S(1)}, u32[]{:S(2)}, u32[]{:S(2)}) collective-permute-start(bf16[20,8,128]{2,1,0:T(8,128)(2,1)S(1)} %get-tuple-element.32), channel_id=1, source_target_pairs={{16,32},{48,64},{80,96},{112,128},{144,160},{176,192},{208,224},{2... | collective-permute-start | bytes 122888 | tf_op jit(solution)/shard_map/ppermute | solution.py:478
  49.0 11.8 %collective-permute-start.3 = (bf16[24,8,128]{2,1,0:T(8,128)(2,1)S(1)}, bf16[24,8,128]{2,1,0:T(8,128)(2,1)S(1)}, u32[]{:S(2)}, u32[]{:S(2)}) collective-permute-start(bf16[24,8,128]{2,1,0:T(8,128)(2,1)S(1)} %get-tuple-element.34), channel_id=1, source_target_pairs={{1,2},{3,4},{5,6},{7,8},{9,10},{11,12},{13,14},{2,1},{4,3},{6,5},{... | collective-permute-start | bytes 147464 | tf_op jit(solution)/shard_map/ppermute | solution.py:483
  66.1 25.2 %all-to-all-start = ((f32[32,4,128]{2,1,0:T(4,128)}), f32[32,4,128]{2,1,0:T(4,128)S(1)}, u32[]{:S(2)}, u32[]{:S(2)}) async-start(f32[32,4,128]{2,1,0:T(4,128)} %bitcast.10), calls=%async_computation | async-start | bytes 131072 | tf_op jit(solution)/shard_map/all_to_all | solution.py:533
